TPU v7x, 32 devices: a whole 2x2x4 slice. The times are simulated.
32 devices in a mesh: ctx: 8 (over y, x, core), head: 4 (over z).
Axes of the slice: x: 2, y: 2, z: 4, core: 2. Of those that a mesh axis runs over, the one named last changes fastest.
Arguments:
- block_order: int32 [16], replicated, may hold values from 0 to 15, as said below
- query_latent: bfloat16 [1024, 128, 576], P('ctx', 'head'), may hold values from -12 to 12
- key_latent: bfloat16 [1024, 576], P('ctx'), may hold values from -6 to 6
- normalizer: float32 [1024, 128], P('ctx', 'head'), may hold values from 6 to 9
- indexer_query: bfloat16 [1024, 64, 128], P('ctx', 'head'), may hold values from -8 to 8
- indexer_key: bfloat16 [1024, 128], P('ctx'), may hold values from -4 to 4
- indexer_weight: bfloat16 [1024, 64], P('ctx', 'head'), may hold values from -4 to 4
Outputs:
- query_grad: float32 [1024, 64, 128], P('ctx', 'head')
- key_grad: float32 [1024, 128], P(('ctx', 'head'))
Inputs may be any that keep to these rules, and one draw needn't show every extreme that they name: `block_order`: entries 2 i and 2 i + 1 are the blocks stored on ctx index i; all entries together are each of 0 to 15 once, and the two entries of one index sum to 15.
All inputs are finite; a program needn't handle non-finite values.
Results may differ from a plain program's by a relative error of at most 0.0037.
Values may be sent and summed in bfloat16 or wider, within the bound.
A program may use at most 128 MiB of HBM per device.

v0:
```python
import math

import jax
import jax.numpy as jnp
from jax import lax
from jax.sharding import PartitionSpec as P

mla_scale = 192.0 ** (-0.5)
loss_scale = 64.0


def gradient(tile_sums, query_pos, key_pos):
    visible = key_pos[None, :] <= query_pos[:, None]
    target_sum = jnp.where(visible, tile_sums[0], 0.0)
    row_total = jnp.sum(target_sum, axis=1, keepdims=True)
    logits = tile_sums[1]
    row_top = jnp.max(jnp.where(visible, logits, -jnp.inf), axis=1, keepdims=True)
    exp_logit = jnp.where(visible, jnp.exp(logits - row_top), 0.0)
    norm_sum = jnp.sum(exp_logit, axis=1, keepdims=True)
    return jnp.where(
        visible, loss_scale * (exp_logit / norm_sum - target_sum / row_total), 0.0
    ).astype(jnp.bfloat16)


def per_device(
    block_order, query_latent, key_latent, normalizer, indexer_query, indexer_key, indexer_weight
):
    query_rows = query_latent.shape[0]
    block_rows = query_rows // 2
    cycle_count = lax.axis_size("ctx")
    group_count = lax.axis_size("head")
    tokens = query_rows * cycle_count
    local_heads = indexer_query.shape[1]
    idx_scale = (local_heads * group_count * indexer_query.shape[2]) ** (-0.5)
    key_pos = (
        block_order[:, None] * block_rows + jnp.arange(block_rows, dtype=jnp.int32)[None, :]
    ).reshape(-1)
    query_pos = lax.dynamic_slice_in_dim(key_pos, lax.axis_index("ctx") * query_rows, query_rows, 0)
    all_latent, all_index = (
        lax.all_gather(key_latent, "ctx", axis=0, tiled=True),
        lax.all_gather(indexer_key, "ctx", axis=0, tiled=True),
    )
    key_block = math.gcd(tokens, 512)
    block_count = tokens // key_block
    weight_float = indexer_weight.astype(jnp.float32)

    def forward(step_index, state):
        tile_sums, positive = state
        offset = step_index * key_block
        latent_block = lax.dynamic_slice_in_dim(all_latent, offset, key_block, 0)
        index_block = lax.dynamic_slice_in_dim(all_index, offset, key_block, 0)
        scores = (
            jnp.einsum(
                "thl,sl->ths", query_latent, latent_block, preferred_element_type=jnp.float32
            )
            * mla_scale
        )
        target_part = jnp.sum(jnp.exp(scores - normalizer[:, :, None]), axis=1)
        idx_dot = jnp.einsum(
            "tjd,sd->tjs", indexer_query, index_block, preferred_element_type=jnp.float32
        )
        logit_part = idx_scale * jnp.sum(
            weight_float[:, :, None] * jnp.maximum(idx_dot, 0.0), axis=1
        )
        tile_sums = lax.dynamic_update_slice_in_dim(
            tile_sums, jnp.stack((target_part, logit_part)), offset, 2
        )
        positive = lax.dynamic_update_slice_in_dim(positive, idx_dot > 0, offset, 2)
        return (tile_sums, positive)

    start_state = (
        jnp.zeros((2, query_rows, tokens), jnp.float32),
        jnp.zeros((query_rows, local_heads, tokens), jnp.bool_),
    )
    tile_sums, positive = lax.fori_loop(0, block_count, forward, start_state)
    share_sums = lax.psum_scatter(tile_sums, "head", scatter_dimension=1, tiled=True)
    share_count = query_rows // group_count
    share_pos = lax.dynamic_slice_in_dim(
        query_pos, lax.axis_index("head") * share_count, share_count, 0
    )
    share_grad = gradient(share_sums, share_pos, key_pos)
    grad_logit = lax.all_gather(share_grad, "head", axis=0, tiled=True)
    weight_scaled = weight_float * idx_scale

    def backward(step_index, state):
        coeff_buffer, query_accum = state
        offset = step_index * key_block
        positive_block = lax.dynamic_slice_in_dim(positive, offset, key_block, 2)
        grad_block = lax.dynamic_slice_in_dim(grad_logit, offset, key_block, 1)
        coeff_block = jnp.where(
            positive_block,
            grad_block.astype(jnp.float32)[:, None, :] * weight_scaled[:, :, None],
            0.0,
        ).astype(jnp.bfloat16)
        index_block = lax.dynamic_slice_in_dim(all_index, offset, key_block, 0)
        query_accum = query_accum + jnp.einsum(
            "tjs,sd->tjd", coeff_block, index_block, preferred_element_type=jnp.float32
        )
        coeff_buffer = lax.dynamic_update_slice_in_dim(coeff_buffer, coeff_block, offset, 2)
        return (coeff_buffer, query_accum)

    back_state = (
        jnp.zeros((query_rows, local_heads, tokens), jnp.bfloat16),
        jnp.zeros(indexer_query.shape, jnp.float32),
    )
    coefficient, query_grad = lax.fori_loop(0, block_count, backward, back_state)
    key_grad = lax.psum_scatter(
        jnp.einsum("tjs,tjd->sd", coefficient, indexer_query, preferred_element_type=jnp.float32),
        ("ctx", "head"),
        scatter_dimension=0,
        tiled=True,
    )
    return (query_grad, key_grad)


def solution(mesh):
    return jax.shard_map(
        per_device,
        mesh=mesh,
        in_specs=(
            P(),
            P("ctx", "head", None),
            P("ctx", None),
            P("ctx", "head"),
            P("ctx", "head", None),
            P("ctx", None),
            P("ctx", "head"),
        ),
        out_specs=(P("ctx", "head", None), P(("ctx", "head"), None)),
        check_vma=False,
    )
```

profile of v0, /device:TPU:0, one launch (start us, length us, event | category | flops | bytes accessed | tf_op | source)
XLA Modules:
  0.0 269.6 jit_solution(7283531578134878488)
XLA Ops:
  7.2 0.0 all-gather.2.cloned.1.call-start
  7.2 0.7 all-gather.2.cloned.1.call-update
  7.9 0.0 reduce-scatter.3.cloned.1.call-start
  8.0 0.7 convert_element_type.20
  8.6 1.2 copy.14
  9.8 11.0 %all_gather.10 = bf16[1024,128]{1,0:T(8,128)(2,1)S(1)} all-gather(bf16[128,128]{1,0:T(8,128)(2,1)} %param.16), channel_id=1, replica_groups=mesh['ctx'=8,'head'=4] {'ctx'}, dimensions={0}, use_global_device_ids=true | all-gather | bytes 294912 | tf_op jit(solution)/shard_map/all_gather | solution.py:41
  20.8 15.8 %all-gather.2.cloned.1.call-done = bf16[1024,576]{0,1:T(8,128)(2,1)} async-done(((bf16[128,576]{0,1:T(8,128)(2,1)}), bf16[1024,576]{0,1:T(8,128)(2,1)}) %all-gather.2.cloned.1.call-update) | async-done | bytes 1179664 | tf_op jit(solution)/shard_map/all_gather | solution.py:40
  36.7 1.1 broadcast_in_dim.49.clone
  37.8 0.8 broadcast_in_dim.50
  38.6 0.0 copy-done.9
  38.6 0.0 copy-start.10
  38.6 0.0 copy-start.8
  38.6 27.1 %while.31 = (s32[]{:T(128)}, f32[2,128,1024]{2,1,0:T(8,128)}, pred[128,16,1024]{0,2,1:T(32,128)(4,1)S(1)}, bf16[1024,576]{0,1:T(8,128)(2,1)}, bf16[128,32,576]{0...) while((s32[]{:T(128)}, f32[2,128,1024]{2,1,0:T(8,128)}, ...), condition=%wide.region_3.0_spmd, body=%wide.region_0.0_spmd.sunk | while | flops 2694905856 | bytes 23814388 | solution.py:75
  38.6 0.0 copy-start
  38.7 6.8 %exponential_reduce_fusion.2 = f32[512,128]{1,0:T(8,128)S(1)} fusion(f32[128,32]{0,1:T(8,128)S(1)} %get-tuple-element.515, bf16[128,32,576]{0,2,1:T(8,128)(2,1)} %get-tuple-element.514, bf16[1024,576]{0,1:T(8,128)(2,1)} %get-tuple-element.513, s32[]{:T(128)S(6)} %select_n.87), kind=kOutput, calls=%fused_computation.clone.1 | convolution fusion | flops 2422145024 | bytes 5586948 | tf_op jit(solution)/shard_map/while/body/eval_jaxpr/thl,sl->ths/dot_general | solution.py:53
  45.5 0.0 copy-done
  45.5 2.7 multiply_reduce_fusion.2
  48.2 0.1 pad_maximum_fusion.2
  48.2 0.2 copy.30
  48.4 0.0 copy-start.1
  48.4 0.9 constant_dynamic-update-slice_fusion.2
  49.3 2.8 %bitcast_dynamic-update-slice_fusion.2 = pred[128,16,1024]{0,2,1:T(32,128)(4,1)S(1)} fusion(pred[128,16,1024]{0,2,1:T(32,128)(4,1)S(1)} %get-tuple-element.499, s32[]{:T(128)S(6)} %select_n.87, f32[512,128,16]{1,0,2:T(8,128)} %get-tuple-element.476), kind=kLoop, calls=%fused_computation.2.clone.1 | loop fusion | flops 1048576 | bytes 5242884 | tf_op jit(solution)/shard_map/while/body/eval_jaxpr/dynamic_update_slice | solution.py:68
  52.2 0.0 copy-start
  52.2 6.8 %exponential_reduce_fusion.2 = f32[512,128]{1,0:T(8,128)S(1)} fusion(f32[128,32]{0,1:T(8,128)S(1)} %get-tuple-element.515, bf16[128,32,576]{0,2,1:T(8,128)(2,1)} %get-tuple-element.514, bf16[1024,576]{0,1:T(8,128)(2,1)} %get-tuple-element.513, s32[]{:T(128)S(6)} %select_n.87), kind=kOutput, calls=%fused_computation.clone.1 | convolution fusion | flops 2422145024 | bytes 5586948 | tf_op jit(solution)/shard_map/while/body/eval_jaxpr/thl,sl->ths/dot_general | solution.py:53
  59.0 2.7 multiply_reduce_fusion.2
  61.7 0.1 pad_maximum_fusion.2
  61.8 0.2 copy.30
  62.0 0.0 copy-start.1
  62.0 0.9 constant_dynamic-update-slice_fusion.2
  62.9 2.8 %bitcast_dynamic-update-slice_fusion.2 = pred[128,16,1024]{0,2,1:T(32,128)(4,1)S(1)} fusion(pred[128,16,1024]{0,2,1:T(32,128)(4,1)S(1)} %get-tuple-element.499, s32[]{:T(128)S(6)} %select_n.87, f32[512,128,16]{1,0,2:T(8,128)} %get-tuple-element.476), kind=kLoop, calls=%fused_computation.2.clone.1 | loop fusion | flops 1048576 | bytes 5242884 | tf_op jit(solution)/shard_map/while/body/eval_jaxpr/dynamic_update_slice | solution.py:68
  65.7 0.0 reduce-scatter.3.cloned.1.call-update
  65.8 0.0 reduce-scatter.5.cloned.1.call-start
  65.8 0.0 copy-done.10
  65.8 0.1 iota_add_fusion
  65.9 0.1 add.94
  66.0 0.1 dynamic_slice.42
  66.1 27.1 %reduce-scatter.3.cloned.1.call-done = f32[2,32,1024]{2,1,0:T(8,128)} async-done(((f32[2,128,1024]{2,1,0:T(8,128)}), f32[2,32,1024]{2,1,0:T(8,128)}) %reduce-scatter.3.cloned.1.call-update) | async-done | bytes 262160 | tf_op jit(solution)/shard_map/reduce_scatter | solution.py:76
  93.2 1.1 fusion.17
  94.3 1.2 fusion.20
  95.5 1.1 fusion.18
  96.6 14.5 %all_gather.11 = bf16[128,1024]{1,0:T(8,128)(2,1)S(1)} all-gather(bf16[32,1024]{1,0:T(8,128)(2,1)S(1)} %fusion.18), channel_id=1, replica_groups=mesh['ctx'=8,'head'=4] {'head'}, dimensions={0}, use_global_device_ids=true | all-gather | bytes 327680 | tf_op jit(solution)/shard_map/all_gather | solution.py:82
  111.0 2.5 broadcast_in_dim.47
  113.5 10.9 %while.32 = (s32[]{:T(128)}, bf16[128,16,1024]{2,0,1:T(8,128)(2,1)}, f32[128,16,128]{2,0,1:T(8,128)}, pred[128,16,1024]{0,2,1:T(32,128)(4,1)S(1)}, bf16[128,1024...) while((s32[]{:T(128)}, ...), condition=%wide.region_9.10_spmd.clone, body=%wide.region_8.9_spmd.clone.sunk | while | flops 275316736 | bytes 53494056 | solution.py:106
  113.6 0.0 copy-start.2
  113.6 0.1 constant_dynamic-slice_fusion.2
  113.6 1.2 copy.31
  114.9 1.0 fusion.36
  115.9 0.2 copy-done.2
  116.1 0.7 fusion.35
  116.8 0.3 copy-done.5
  117.1 1.9 copy-done.3
  119.0 0.0 copy-start.2
  119.0 0.1 constant_dynamic-slice_fusion.2
  119.1 1.2 copy.31
  120.3 0.0 copy-done.4
  120.4 1.0 fusion.36
  121.4 0.1 copy-done.2
  121.5 0.7 fusion.35
  122.2 0.3 copy-done.5
  122.5 1.9 copy-done.3
  124.4 4.4 %convolution_bitcast_fusion = f32[1024,128]{1,0:T(8,128)} fusion(bf16[128,16,1024]{2,0,1:T(8,128)(2,1)} %get-tuple-element.285, bf16[128,16,128]{2,1,0:T(8,128)(2,1)S(1)} %copy-done.7), kind=kOutput, calls=%fused_computation.26 | convolution fusion | flops 536870912 | bytes 5242880 | tf_op jit(solution)/shard_map/tjs,tjd->sd/dot_general | solution.py:108
  128.8 0.0 reduce-scatter.5.cloned.1.call-update
  128.8 1.6 copy.19
  130.4 132.7 %reduce-scatter.5.cloned.1.call-done = f32[32,128]{1,0:T(8,128)} async-done(((f32[1024,128]{1,0:T(8,128)}), f32[32,128]{1,0:T(8,128)}) %reduce-scatter.5.cloned.1.call-update) | async-done | bytes 16400 | tf_op jit(solution)/shard_map/reduce_scatter | solution.py:107
  (23 shorter events, 0.1 us)
Async XLA Ops:
  7.2 31.4 %copy-start.9 = (f32[128,32]{0,1:T(8,128)S(1)}, f32[128,32]{0,1:T(8,128)}, u32[]{:S(2)}) copy-start(f32[128,32]{0,1:T(8,128)} %param.14) | copy-start | bytes 49156
  7.2 29.5 %all-gather.2.cloned.1.call-start = ((), (), s32[]{:S(2)}) async-start(), calls=%async_computation.2 | async-start | bytes 1327104 | tf_op jit(solution)/shard_map/all_gather | solution.py:40
  7.9 85.3 %reduce-scatter.3.cloned.1.call-start = ((), (), s32[]{:S(2)}) async-start(), calls=%async_computation.3 | async-start | bytes 1310720 | tf_op jit(solution)/shard_map/reduce_scatter | solution.py:76
  38.6 27.2 %copy-start.10 = (s32[16]{0:T(128)S(1)}, s32[16]{0:T(128)}, u32[]{:S(2)}) copy-start(s32[16]{0:T(128)} %param.11) | copy-start | bytes 196
  38.6 27.5 %copy-start.8 = (bf16[128,16]{0,1:T(8,128)(2,1)S(1)}, bf16[128,16]{0,1:T(8,128)(2,1)}, u32[]{:S(2)}) copy-start(bf16[128,16]{0,1:T(8,128)(2,1)} %param.17) | copy-start | bytes 12292
  38.6 6.8 %copy-start = (bf16[128,16,128]{2,0,1:T(8,128)(2,1)}, bf16[128,16,128]{2,0,1:T(8,128)(2,1)S(1)}, u32[]{:S(2)}) copy-start(bf16[128,16,128]{2,0,1:T(8,128)(2,1)S(1)} %get-tuple-element.518) | copy-start | bytes 1572868 | tf_op jit(solution)/shard_map/while
  48.4 3.7 %copy-start.1 = (bf16[128,16,128]{2,0,1:T(8,128)(2,1)S(1)}, bf16[128,16,128]{2,0,1:T(8,128)(2,1)}, u32[]{:S(2)}) copy-start(bf16[128,16,128]{2,0,1:T(8,128)(2,1)} %copy-done) | copy-start | bytes 1572868 | tf_op jit(solution)/shard_map/while
  52.2 6.8 %copy-start = (bf16[128,16,128]{2,0,1:T(8,128)(2,1)}, bf16[128,16,128]{2,0,1:T(8,128)(2,1)S(1)}, u32[]{:S(2)}) copy-start(bf16[128,16,128]{2,0,1:T(8,128)(2,1)S(1)} %get-tuple-element.518) | copy-start | bytes 1572868 | tf_op jit(solution)/shard_map/while
  62.0 3.7 %copy-start.1 = (bf16[128,16,128]{2,0,1:T(8,128)(2,1)S(1)}, bf16[128,16,128]{2,0,1:T(8,128)(2,1)}, u32[]{:S(2)}) copy-start(bf16[128,16,128]{2,0,1:T(8,128)(2,1)} %copy-done) | copy-start | bytes 1572868 | tf_op jit(solution)/shard_map/while
  65.8 197.3 %reduce-scatter.5.cloned.1.call-start = ((), (), s32[]{:S(2)}) async-start(), calls=%async_computation.4 | async-start | bytes 540672 | tf_op jit(solution)/shard_map/reduce_scatter | solution.py:107
  113.5 10.9 %copy-start.7 = (bf16[128,16,128]{2,1,0:T(8,128)(2,1)S(1)}, bf16[128,16,128]{2,1,0:T(8,128)(2,1)}, u32[]{:S(2)}) copy-start(bf16[128,16,128]{2,1,0:T(8,128)(2,1)} %param.15) | copy-start | bytes 1572868
  113.5 1.3 copy-start.4
  113.6 2.5 copy-start.2
  116.1 1.0 copy-start.5
  117.1 1.9 copy-start.3
  119.0 1.3 copy-start.4
  119.0 2.5 copy-start.2
  121.5 1.0 copy-start.5
  122.5 1.9 copy-start.3
  124.4 4.4 %copy-start.6 = (f32[128,16,128]{2,0,1:T(8,128)S(1)}, f32[128,16,128]{2,0,1:T(8,128)}, u32[]{:S(2)}) copy-start(f32[128,16,128]{2,0,1:T(8,128)} %get-tuple-element.344) | copy-start | bytes 3145732
Sparse Core Ops, SparseCore 0:
  9.9 26.7 all-gather.1
  65.9 27.2 reduce-scatter.2
  128.9 134.0 reduce-scatter.4
where the time goes:
time: 270 us
  waiting for transfers between devices  176 us (65%)
  blocking collectives  25.5 us (9%)
  matrix products  25.3 us (9%)
  local copies, waits for them, and re-layouts  16.9 us (6%)
  between operations  13.8 us (5%)
  other arithmetic  11.4 us (4%)
    reduce_scatter x1, waiting for transfers between devices, per_device(): lax.psum_scatter(jnp.einsum('tjs,tjd->sd', coefficient, indexer_query, pr...  133 us
    reduce_scatter x1, waiting for transfers between devices, per_device(): lax.psum_scatter(tile_sums, 'head', scatter_dimension=1, tiled=True)  27.1 us
    all_gather x1, waiting for transfers between devices, per_device(): lax.all_gather(key_latent, 'ctx', axis=0, tiled=True)  15.8 us
    all_gather x1, blocking collectives, per_device(): grad_logit = lax.all_gather(share_grad, 'head', axis=0, tiled=True)  14.5 us
    dot_general x2, matrix products, forward(): jnp.einsum('thl,sl->ths', query_latent, latent_block, preferred_element_t...  13.6 us
    all_gather x1, blocking collectives, per_device(): lax.all_gather(indexer_key, 'ctx', axis=0, tiled=True)  11 us
    dynamic_update_slice x2, other arithmetic, forward(): positive = lax.dynamic_update_slice_in_dim(positive, idx_dot > 0, offset, 2)  5.67 us
  transfers between devices with their start and end apart: 3, of which 3 were waited for; matrix products, arithmetic and copies ran while one was open for 1% of the time, Pallas kernels for 0%

commit v1 on v0

v1 whole, which is shorter than its diff:
```python
import functools
import math

import jax
import jax.numpy as jnp
from jax import lax
from jax.experimental import pallas as pl
from jax.experimental.pallas import tpu as pltpu
from jax.sharding import PartitionSpec as P

MESH = pl.DeviceIdType.MESH
mla_scale = 192.0 ** (-0.5)
loss_scale = 64.0
log2e = math.log2(math.e)
NT_DIMS = (((1,), (1,)), ((), ()))
TN_DIMS = (((0,), (0,)), ((), ()))


def enter(groups, shares):
    ctx, head = lax.axis_index("ctx"), lax.axis_index("head")
    group, core = ctx // 2, lax.rem(ctx, 2)
    barrier = pltpu.get_barrier_semaphore()
    count = 0
    if groups:
        for step in range(1, groups):
            peer = lax.rem(group + step, groups) * 2 + core
            pl.semaphore_signal(barrier, 1, device_id={"ctx": peer}, device_id_type=MESH)
        pl.semaphore_signal(
            barrier, 1, device_id={"ctx": group * 2 + 1 - core}, device_id_type=MESH
        )
        count += groups
    for step in range(1, shares):
        peer = lax.rem(head + step, shares)
        pl.semaphore_signal(barrier, 1, device_id={"head": peer}, device_id_type=MESH)
    count += shares - 1
    pl.semaphore_wait(barrier, count)


def remote(src, dst, send, recv, device):
    return pltpu.make_async_remote_copy(
        src_ref=src, dst_ref=dst, send_sem=send, recv_sem=recv, device_id=device, device_id_type=MESH
    )


def gather_kernel(
    groups, shares, lat, idx, iq, iw, all_lat, all_idx, iq_recv, iw_recv,
    local, qs, qr, ws, wr, ds, dr, fs, fr,
):
    ctx, head = lax.axis_index("ctx"), lax.axis_index("head")
    group, core = ctx // 2, lax.rem(ctx, 2)
    sibling = group * 2 + 1 - core
    rows = lat.shape[0]
    half = rows // 2
    share = half // shares
    own = [
        pltpu.make_async_copy(lat, all_lat.at[ctx], local.at[0]),
        pltpu.make_async_copy(idx, all_idx.at[ctx], local.at[1]),
    ]
    for e in range(2):
        take = pl.ds(pl.multiple_of(e * half + head * share, share), share)
        own.append(pltpu.make_async_copy(iq.at[take], iq_recv.at[head, e], local.at[2 + e]))
        own.append(pltpu.make_async_copy(iw.at[take], iw_recv.at[head, e], local.at[4 + e]))
    for copy in own:
        copy.start()
    enter(groups, shares)
    sent = []
    for step in range(1, groups):
        peer = lax.rem(group + step, groups) * 2 + core
        for k, (src, dst) in enumerate(((lat, all_lat), (idx, all_idx))):
            copy = remote(src, dst.at[ctx], ds.at[k, step], dr.at[k, step], {"ctx": peer})
            copy.start()
            sent.append(copy)
    for k, (src, dst) in enumerate(((lat, all_lat), (idx, all_idx))):
        copy = remote(src, dst.at[ctx], fs.at[k, 0], fr.at[k, 0], {"ctx": sibling})
        copy.start()
        sent.append(copy)
    for step in range(1, shares):
        peer = lax.rem(head + step, shares)
        for e in range(2):
            take = pl.ds(pl.multiple_of(e * half + peer * share, share), share)
            for src, dst, s, r in ((iq, iq_recv, qs, qr), (iw, iw_recv, ws, wr)):
                copy = remote(
                    src.at[take], dst.at[head, e], s.at[step, e], r.at[step, e], {"head": peer}
                )
                copy.start()
                sent.append(copy)
    for step in range(1, groups):
        source = lax.rem(group + groups - step, groups) * 2 + core
        for k, dst in enumerate((all_lat, all_idx)):
            slot = dst.at[source]
            remote(slot, slot, ds.at[k, step], dr.at[k, step], {"ctx": sibling}).wait_recv()
            copy = remote(slot, slot, fs.at[k, step], fr.at[k, step], {"ctx": sibling})
            copy.start()
            sent.append(copy)
    for step in range(groups):
        source = lax.rem(group + groups - step, groups) * 2 + 1 - core
        for k, dst in enumerate((all_lat, all_idx)):
            slot = dst.at[source]
            remote(slot, slot, fs.at[k, step], fr.at[k, step], {"ctx": sibling}).wait_recv()
    for step in range(1, shares):
        source = lax.rem(head + shares - step, shares)
        for e in range(2):
            for dst, s, r in ((iq_recv, qs, qr), (iw_recv, ws, wr)):
                slot = dst.at[source, e]
                remote(slot, slot, s.at[step, e], r.at[step, e], {"head": source}).wait_recv()
    for copy in sent:
        copy.wait_send()
    for copy in own:
        copy.wait()


def gather(lat, idx, iq, iw, cycle, shares):
    groups = cycle // 2
    rows = lat.shape[0]
    share = rows // 2 // shares
    dma = pltpu.SemaphoreType.DMA
    return pl.pallas_call(
        functools.partial(gather_kernel, groups, shares),
        out_shape=(
            jax.ShapeDtypeStruct((cycle,) + lat.shape, lat.dtype),
            jax.ShapeDtypeStruct((cycle,) + idx.shape, idx.dtype),
            jax.ShapeDtypeStruct((shares, 2, share) + iq.shape[1:], iq.dtype),
            jax.ShapeDtypeStruct((shares, 2, share) + iw.shape[1:], iw.dtype),
        ),
        in_specs=[pl.BlockSpec(memory_space=pl.ANY)] * 4,
        out_specs=[pl.BlockSpec(memory_space=pltpu.VMEM)] * 4,
        scratch_shapes=[
            dma((6,)),
            dma((shares, 2)), dma((shares, 2)), dma((shares, 2)), dma((shares, 2)),
            dma((2, groups)), dma((2, groups)), dma((2, groups)), dma((2, groups)),
        ],
        compiler_params=pltpu.CompilerParams(collective_id=0, has_side_effects=True),
        name="gather",
    )(lat, idx, iq, iw)


def forward_kernel(
    shares, tile, order, q, norm, lat, idx, iq, iw, sums, probs, idx_sorted, lat_sorted, logits
):
    step, steps = pl.program_id(0), pl.num_programs(0)
    ctx, head = lax.axis_index("ctx"), lax.axis_index("head")
    blocks = order.shape[0]
    half = lat.shape[0] // blocks
    tokens = lat.shape[0]
    tiles = tokens // tile
    share = half // shares
    heads = q.shape[1]
    idx_heads = iq.shape[3]
    idx_scale = (idx_heads * shares * iq.shape[4]) ** (-0.5)

    @pl.when(step == 0)
    def _():
        def sort(r, carry):
            src = pl.ds(pl.multiple_of(r * half, half), half)
            dst = pl.ds(pl.multiple_of(order[r] * half, half), half)
            lat_sorted[dst, :] = lat[src, :]
            idx_sorted[dst, :] = idx[src, :]
            return carry

        lax.fori_loop(0, blocks, sort, 0)
        for e in range(2):
            block = order[2 * ctx + e]
            slot = (block >= blocks // 2).astype(jnp.int32)
            first = block * half + head * share
            logits[...] = jnp.full(logits.shape, -jnp.inf, jnp.float32)
            weights = [
                jnp.broadcast_to(
                    (iw[z, e].astype(jnp.float32) * idx_scale)[:, :, None], (share, idx_heads, 128)
                )
                for z in range(shares)
            ]

            def logit_tile(k, carry):
                cols = pl.ds(pl.multiple_of(k * tile, tile), tile)
                keys = idx_sorted[cols, :]
                total = jnp.zeros((share, tile), jnp.float32)
                for z in range(shares):
                    dots = lax.dot_general(
                        iq[z, e].reshape(share * idx_heads, -1), keys, NT_DIMS,
                        preferred_element_type=jnp.float32,
                    ).reshape(share, idx_heads, tile)
                    parts = [
                        jnp.sum(weights[z] * jnp.maximum(dots[:, :, c : c + 128], 0.0), axis=1)
                        for c in range(0, tile, 128)
                    ]
                    total = total + jnp.concatenate(parts, axis=1)
                shape = (share, tile)
                visible = k * tile + lax.broadcasted_iota(
                    jnp.int32, shape, 1
                ) <= first + lax.broadcasted_iota(jnp.int32, shape, 0)
                logits[:, cols] = jnp.where(visible, total, -jnp.inf)
                return carry

            lax.fori_loop(0, (block * half + half - 1) // tile + 1, logit_tile, 0)
            values = logits[...]
            top = jnp.max(values, axis=1, keepdims=True)
            expo = jnp.exp(values - top)
            norm_sum = jnp.sum(expo, axis=1, keepdims=True)
            probs[pl.ds(pl.multiple_of(slot * share, share), share), :] = expo / norm_sum

    chunk = q.shape[0]
    per_block = half // chunk
    e = step // per_block
    inner = lax.rem(step, per_block)
    block = order[2 * ctx + e]
    slot = (block >= blocks // 2).astype(jnp.int32)
    out_rows = pl.ds(pl.multiple_of(slot * half + inner * chunk, chunk), chunk)
    first = block * half + inner * chunk
    queries = q[...].reshape(chunk * heads, q.shape[2])
    shift = jnp.broadcast_to((norm[...] * log2e)[:, :, None], (chunk, heads, 128))
    count = (block * half + half - 1) // tile + 1

    def score_tile(k, carry):
        cols = pl.ds(pl.multiple_of(k * tile, tile), tile)
        scores = lax.dot_general(
            queries, lat_sorted[cols, :], NT_DIMS, preferred_element_type=jnp.float32
        ).reshape(chunk, heads, tile)
        parts = [
            jnp.sum(
                jnp.exp2(scores[:, :, c : c + 128] * (mla_scale * log2e) - shift), axis=1
            )
            for c in range(0, tile, 128)
        ]
        total = jnp.concatenate(parts, axis=1)
        shape = (chunk, tile)
        visible = k * tile + lax.broadcasted_iota(
            jnp.int32, shape, 1
        ) <= first + lax.broadcasted_iota(jnp.int32, shape, 0)
        sums[out_rows, cols] = jnp.where(visible, total, 0.0)
        return carry

    lax.fori_loop(0, count, score_tile, 0)

    def clear(k, carry):
        cols = pl.ds(pl.multiple_of(k * tile, tile), tile)
        sums[out_rows, cols] = jnp.zeros((chunk, tile), jnp.float32)
        return carry

    lax.fori_loop(count, tiles, clear, 0)


def forward(order, q, norm, lat, idx, iq, iw, shares):
    rows, heads, width = q.shape
    tokens = lat.shape[0]
    half = rows // 2
    share = half // shares
    chunk = 16
    tile = 256
    whole = lambda a: pl.BlockSpec(a.shape, lambda i, o: (0,) * a.ndim)
    return pl.pallas_call(
        functools.partial(forward_kernel, shares, tile),
        out_shape=(
            jax.ShapeDtypeStruct((rows, tokens), jnp.float32),
            jax.ShapeDtypeStruct((2 * share, tokens), jnp.float32),
            jax.ShapeDtypeStruct(idx.shape, idx.dtype),
        ),
        grid_spec=pltpu.PrefetchScalarGridSpec(
            num_scalar_prefetch=1,
            grid=(rows // chunk,),
            in_specs=[
                pl.BlockSpec((chunk, heads, width), lambda i, o: (i, 0, 0)),
                pl.BlockSpec((chunk, heads), lambda i, o: (i, 0)),
                whole(lat), whole(idx), whole(iq), whole(iw),
            ],
            out_specs=[
                pl.BlockSpec((rows, tokens), lambda i, o: (0, 0)),
                pl.BlockSpec((2 * share, tokens), lambda i, o: (0, 0)),
                pl.BlockSpec(idx.shape, lambda i, o: (0, 0)),
            ],
            scratch_shapes=[
                pltpu.VMEM(lat.shape, lat.dtype),
                pltpu.VMEM((share, tokens), jnp.float32),
            ],
        ),
        name="forward",
    )(order, q, norm, lat, idx, iq, iw)


def gradient_kernel(shares, sums, probs, grad, low, high, ls, lr, hs, hr, gs, gr):
    head = lax.axis_index("head")
    rows, tokens = sums.shape
    half = rows // 2
    share = half // shares
    short = tokens // 2
    enter(0, shares)
    sent = []
    for step in range(1, shares):
        peer = lax.rem(head + step, shares)
        start = pl.multiple_of(peer * share, share)
        for copy in (
            remote(
                sums.at[pl.ds(start, share), pl.ds(0, short)], low.at[step], ls.at[step],
                lr.at[step], {"head": peer},
            ),
            remote(
                sums.at[pl.ds(half + start, share)], high.at[step], hs.at[step], hr.at[step],
                {"head": peer},
            ),
        ):
            copy.start()
            sent.append(copy)
    start = pl.multiple_of(head * share, share)
    total_low = sums[pl.ds(start, share), :short]
    total_high = sums[pl.ds(half + start, share), :]
    for step in range(1, shares):
        source = lax.rem(head + shares - step, shares)
        remote(low.at[step], low.at[step], ls.at[step], lr.at[step], {"head": source}).wait_recv()
        total_low = total_low + low[step]
        remote(high.at[step], high.at[step], hs.at[step], hr.at[step], {"head": source}).wait_recv()
        total_high = total_high + high[step]
    row_low = jnp.sum(total_low, axis=1, keepdims=True)
    row_high = jnp.sum(total_high, axis=1, keepdims=True)
    grad[head, 0, :, :short] = (
        loss_scale * (probs[:share, :short] - total_low / row_low)
    ).astype(jnp.bfloat16)
    grad[head, 1] = (loss_scale * (probs[share:, :] - total_high / row_high)).astype(jnp.bfloat16)
    for step in range(1, shares):
        peer = lax.rem(head + step, shares)
        for copy in (
            remote(
                grad.at[head, 0, :, pl.ds(0, short)], grad.at[head, 0, :, pl.ds(0, short)],
                gs.at[0, step], gr.at[0, step], {"head": peer},
            ),
            remote(
                grad.at[head, 1], grad.at[head, 1], gs.at[1, step], gr.at[1, step], {"head": peer}
            ),
        ):
            copy.start()
            sent.append(copy)
    for step in range(1, shares):
        source = lax.rem(head + shares - step, shares)
        slot = grad.at[source, 0, :, pl.ds(0, short)]
        remote(slot, slot, gs.at[0, step], gr.at[0, step], {"head": source}).wait_recv()
        slot = grad.at[source, 1]
        remote(slot, slot, gs.at[1, step], gr.at[1, step], {"head": source}).wait_recv()
    for copy in sent:
        copy.wait_send()


def gradient(sums, probs, shares):
    rows, tokens = sums.shape
    share = rows // 2 // shares
    dma = pltpu.SemaphoreType.DMA
    return pl.pallas_call(
        functools.partial(gradient_kernel, shares),
        out_shape=jax.ShapeDtypeStruct((shares, 2, share, tokens), jnp.bfloat16),
        in_specs=[pl.BlockSpec(memory_space=pltpu.VMEM)] * 2,
        out_specs=pl.BlockSpec(memory_space=pltpu.VMEM),
        scratch_shapes=[
            pltpu.VMEM((shares, share, tokens // 2), jnp.float32),
            pltpu.VMEM((shares, share, tokens), jnp.float32),
            dma((shares,)), dma((shares,)), dma((shares,)), dma((shares,)),
            dma((2, shares)), dma((2, shares)),
        ],
        compiler_params=pltpu.CompilerParams(collective_id=1, has_side_effects=True),
        name="gradient",
    )(sums, probs)


def backward_kernel(shares, tile, order, iq, iw, grad, idx, query_grad, key_grad, total):
    step, steps = pl.program_id(0), pl.num_programs(0)
    ctx = lax.axis_index("ctx")
    blocks = order.shape[0]
    tokens = idx.shape[0]
    half = tokens // blocks
    share, heads, dim = iq.shape
    idx_scale = (heads * shares * dim) ** (-0.5)

    @pl.when(step == 0)
    def _():
        total[...] = jnp.zeros_like(total)

    e = step // shares
    part = lax.rem(step, shares)
    block = order[2 * ctx + e]
    slot = (block >= blocks // 2).astype(jnp.int32)
    queries = iq[...].reshape(share * heads, dim)
    weights = jnp.broadcast_to(
        (iw[...].astype(jnp.float32) * idx_scale)[:, :, None], (share, heads, 128)
    )
    query_grad[...] = jnp.zeros_like(query_grad)

    def grad_tile(k, carry):
        cols = pl.ds(pl.multiple_of(k * tile, tile), tile)
        keys = idx[cols, :]
        dots = lax.dot_general(
            queries, keys, NT_DIMS, preferred_element_type=jnp.float32
        ).reshape(share, heads, tile)
        rate = grad[part, slot, :, cols].astype(jnp.float32)
        parts = [
            jnp.where(
                dots[:, :, c : c + 128] > 0, rate[:, None, c : c + 128] * weights, 0.0
            )
            for c in range(0, tile, 128)
        ]
        coefficient = (
            jnp.concatenate(parts, axis=2).reshape(share * heads, tile).astype(jnp.bfloat16)
        )
        query_grad[...] += jnp.dot(
            coefficient, keys, preferred_element_type=jnp.float32
        ).reshape(share, heads, dim)
        total[cols, :] += lax.dot_general(
            coefficient, queries, TN_DIMS, preferred_element_type=jnp.float32
        )
        return carry

    lax.fori_loop(0, (block * half + half - 1) // tile + 1, grad_tile, 0)

    @pl.when(step == steps - 1)
    def _():
        def store(r, carry):
            dst = pl.ds(pl.multiple_of(r * half, half), half)
            src = pl.ds(pl.multiple_of(order[r] * half, half), half)
            key_grad[dst, :] = total[src, :]
            return carry

        lax.fori_loop(0, blocks, store, 0)


def backward(order, iq, iw, grad, idx, shares):
    rows, heads, dim = iq.shape
    share = rows // 2 // shares
    tile = 256
    return pl.pallas_call(
        functools.partial(backward_kernel, shares, tile),
        out_shape=(
            jax.ShapeDtypeStruct(iq.shape, jnp.float32),
            jax.ShapeDtypeStruct(idx.shape, jnp.float32),
        ),
        grid_spec=pltpu.PrefetchScalarGridSpec(
            num_scalar_prefetch=1,
            grid=(2 * shares,),
            in_specs=[
                pl.BlockSpec((share, heads, dim), lambda i, o: (i, 0, 0)),
                pl.BlockSpec((share, heads), lambda i, o: (i, 0)),
                pl.BlockSpec(grad.shape, lambda i, o: (0, 0, 0, 0)),
                pl.BlockSpec(idx.shape, lambda i, o: (0, 0)),
            ],
            out_specs=[
                pl.BlockSpec((share, heads, dim), lambda i, o: (i, 0, 0)),
                pl.BlockSpec(idx.shape, lambda i, o: (0, 0)),
            ],
            scratch_shapes=[pltpu.VMEM(idx.shape, jnp.float32)],
        ),
        name="backward",
    )(order, iq, iw, grad, idx)


def reduce_kernel(groups, shares, parts, out, near, mid, far, acc, last, ns, nr, ms, mr, fs, fr):
    ctx, head = lax.axis_index("ctx"), lax.axis_index("head")
    group, core = ctx // 2, lax.rem(ctx, 2)
    sibling = group * 2 + 1 - core
    rows = out.shape[0]
    enter(groups, shares)
    sent = []
    for step in [*range(1, groups), 0]:
        peer = lax.rem(group + step, groups)
        copy = remote(
            parts.at[peer * 2 + 1 - core], near.at[step], ns.at[step], nr.at[step], {"ctx": sibling}
        )
        copy.start()
        sent.append(copy)
    for step in range(1, groups):
        peer = lax.rem(group + step, groups)
        remote(near.at[step], near.at[step], ns.at[step], nr.at[step], {"ctx": sibling}).wait_recv()
        acc[step] = parts[peer * 2 + core] + near[step]
        copy = remote(
            acc.at[step], mid.at[step], ms.at[step], mr.at[step], {"ctx": peer * 2 + core}
        )
        copy.start()
        sent.append(copy)
    remote(near.at[0], near.at[0], ns.at[0], nr.at[0], {"ctx": sibling}).wait_recv()
    value = parts[ctx] + near[0]
    for step in range(1, groups):
        remote(mid.at[step], mid.at[step], ms.at[step], mr.at[step], {"ctx": sibling}).wait_recv()
        value = value + mid[step]
    last[...] = value
    for step in range(1, shares):
        peer = lax.rem(head + step, shares)
        copy = remote(
            last.at[pl.ds(pl.multiple_of(peer * rows, rows), rows)], far.at[step], fs.at[step],
            fr.at[step], {"head": peer},
        )
        copy.start()
        sent.append(copy)
    value = last[pl.ds(pl.multiple_of(head * rows, rows), rows), :]
    for step in range(1, shares):
        remote(far.at[step], far.at[step], fs.at[step], fr.at[step], {"head": head}).wait_recv()
        value = value + far[step]
    out[...] = value
    for copy in sent:
        copy.wait_send()


def reduce(parts, cycle, shares):
    groups = cycle // 2
    rows, dim = parts.shape[0] // cycle, parts.shape[1]
    dma = pltpu.SemaphoreType.DMA
    buffer = pltpu.VMEM((groups, rows, dim), jnp.float32)
    return pl.pallas_call(
        functools.partial(reduce_kernel, groups, shares),
        out_shape=jax.ShapeDtypeStruct((rows // shares, dim), jnp.float32),
        in_specs=[pl.BlockSpec(memory_space=pltpu.VMEM)],
        out_specs=pl.BlockSpec(memory_space=pltpu.VMEM),
        scratch_shapes=[
            buffer, buffer, pltpu.VMEM((shares, rows // shares, dim), jnp.float32), buffer,
            pltpu.VMEM((rows, dim), jnp.float32),
            dma((groups,)), dma((groups,)), dma((groups,)), dma((groups,)),
            dma((shares,)), dma((shares,)),
        ],
        compiler_params=pltpu.CompilerParams(collective_id=2, has_side_effects=True),
        name="reduce",
    )(parts.reshape(cycle, rows, dim))


def per_device(
    block_order, query_latent, key_latent, normalizer, indexer_query, indexer_key, indexer_weight
):
    cycle, shares = lax.axis_size("ctx"), lax.axis_size("head")
    lat, idx, iq, iw = gather(
        key_latent, indexer_key, indexer_query, indexer_weight, cycle, shares
    )
    lat = lat.reshape(-1, lat.shape[2])
    idx = idx.reshape(-1, idx.shape[2])
    sums, probs, idx_sorted = forward(
        block_order, query_latent, normalizer, lat, idx, iq, iw, shares
    )
    grad = gradient(sums, probs, shares)
    query_grad, key_parts = backward(
        block_order, indexer_query, indexer_weight, grad, idx_sorted, shares
    )
    return query_grad, reduce(key_parts, cycle, shares)


def solution(mesh):
    return jax.shard_map(
        per_device,
        mesh=mesh,
        in_specs=(
            P(),
            P("ctx", "head", None),
            P("ctx", None),
            P("ctx", "head"),
            P("ctx", "head", None),
            P("ctx", None),
            P("ctx", "head"),
        ),
        out_specs=(P("ctx", "head", None), P(("ctx", "head"), None)),
        check_vma=False,
    )
```

time: 270 us -> 97.5 us (0.36)
  waiting for transfers between devices: 176 us -> 0 us
  Pallas kernels: 0 us -> 81.8 us
  blocking collectives: 25.5 us -> 0 us
  matrix products: 25.3 us -> 0 us
  between operations: 13.8 us -> 0.66 us
  other arithmetic: 11.4 us -> 0 us
    reduce_scatter x2 -> x0, waiting for transfers between devices: 160 us -> none  [the longest x1 133 us: per_device(): lax.psum_scatter(jnp.einsum('tjs,tjd->sd', coefficient, indexer_query, pr...]
    pallas_call x0 -> x5, Pallas kernels: none -> 81.8 us  [the longest x1 19.3 us: gather(): pl.pallas_call(functools.partial(gather_kernel, groups, shares), out_shap...]
    all_gather x2 -> x0, blocking collectives: 25.5 us -> none  [the longest x1 14.5 us: per_device(): grad_logit = lax.all_gather(share_grad, 'head', axis=0, tiled=True)]
    dot_general x7 -> x0, matrix products: 25.3 us -> none  [the longest x2 13.6 us: forward(): jnp.einsum('thl,sl->ths', query_latent, latent_block, preferred_element_t...]
    all_gather x1 -> x0, waiting for transfers between devices: 15.8 us -> none  [per_device(): lax.all_gather(key_latent, 'ctx', axis=0, tiled=True)]
    unnamed x11 -> x5, local copies, waits for them, and re-layouts: 1.61 us -> 14.8 us
    dynamic_update_slice x4 -> x0, other arithmetic: 7.02 us -> none  [the longest x2 5.67 us: forward(): positive = lax.dynamic_update_slice_in_dim(positive, idx_dot > 0, offset, 2)]
    while x25 -> x0, local copies, waits for them, and re-layouts: 6 us -> none
  transfers between devices with their start and end apart: 3 -> 0, of which waited for: 3 -> 0; matrix products, arithmetic and copies ran while one was open for 1% -> 0% of each run, Pallas kernels for 0% -> 0%
where the time goes in v1:
time: 97.5 us; the launch traced here: 97.3 us
  Pallas kernels  81.8 us (84%)
  local copies, waits for them, and re-layouts  14.8 us (15%)
    pallas_call x1, Pallas kernels, gather(): pl.pallas_call(functools.partial(gather_kernel, groups, shares), out_shap...  19.3 us
    pallas_call x1, Pallas kernels, gradient(): pl.pallas_call(functools.partial(gradient_kernel, shares), out_shape=jax....  19 us
    pallas_call x1, Pallas kernels, forward(): pl.pallas_call(functools.partial(forward_kernel, shares, tile), out_shape...  17.1 us
    unnamed x5, local copies, waits for them, and re-layouts  14.8 us
    pallas_call x1, Pallas kernels, backward(): pl.pallas_call(functools.partial(backward_kernel, shares, tile), out_shap...  13.3 us
    pallas_call x1, Pallas kernels, reduce(): pl.pallas_call(functools.partial(reduce_kernel, groups, shares), out_shap...  13.1 us

profile of v1, /device:TPU:0, one launch (start us, length us, event | category | flops | bytes accessed | tf_op | source)
XLA Modules:
  0.0 97.3 jit_solution(15252461293501021023)
XLA Ops:
  0.6 1.4 %copy.13.iw = bf16[128,16]{1,0:T(8,128)(2,1)} copy(bf16[128,16]{0,1:T(8,128)(2,1)} %param.13) | data formatting | bytes 8192 | tf_op args[6]
  2.0 1.4 %copy.12.norm = f32[128,32]{1,0:T(8,128)} copy(f32[128,32]{0,1:T(8,128)} %param.10) | data formatting | bytes 32768 | tf_op args[3]
  3.5 1.7 %copy.9.lat = bf16[128,576]{1,0:T(8,128)(2,1)} copy(bf16[128,576]{0,1:T(8,128)(2,1)} %param.9) | data formatting | bytes 294912 | tf_op args[2]
  5.2 19.3 %gather.1 = (bf16[8,128,576]{2,1,0:T(8,128)(2,1)}, bf16[8,128,128]{2,1,0:T(8,128)(2,1)}, bf16[4,2,16,16,128]{4,3,2,1,0:T(8,128)(2,1)}, bf16[4,2,16,16]{3,2,1,0:T(8,128)(2,1)}) custom-call(bf16[128,576]{1,0:T(8,128)(2,1)} %copy.9.lat, bf16[128,128]{1,0:T(8,128)(2,1)} %idx.1, bf16[128,16,128]{2,1,0:T(8,128)(2,1)} %iq.3, bf16[128,16]{1,0:T(8,128)(2,1)} %copy.13.iw), custom_call_target="tpu_custom_call" | custom-call | tf_op jit(solution)/shard_map/gather/pallas_call | solution.py:117
  24.4 9.0 %copy.11.q = bf16[128,32,576]{2,1,0:T(8,128)(2,1)} copy(bf16[128,32,576]{0,2,1:T(8,128)(2,1)} %param.8) | data formatting | bytes 9437184 | tf_op args[1]
  33.4 17.1 %forward.1 = (f32[128,1024]{1,0:T(8,128)}, f32[32,1024]{1,0:T(8,128)}, bf16[1024,128]{1,0:T(8,128)(2,1)}) custom-call(s32[16]{0:T(128)} %order.3, bf16[128,32,576]{2,1,0:T(8,128)(2,1)} %copy.11.q, f32[128,32]{1,0:T(8,128)} %copy.12.norm, bf16[1024,576]{1,0:T(8,128)(2,1)} %bitcast.3, bf16[1024,128]{1,0:T(8,128)(2,1)} %bitcast.5, ...), custom_call_target="tpu_custom_call" | custom-call | tf_op jit(solution)/shard_map/forward/pallas_call | solution.py:250
  50.5 19.0 %gradient.1.grad = bf16[4,2,16,1024]{3,2,1,0:T(8,128)(2,1)} custom-call(f32[128,1024]{1,0:T(8,128)} %get-tuple-element.15.sums, f32[32,1024]{1,0:T(8,128)} %get-tuple-element.16.probs), custom_call_target="tpu_custom_call" | custom-call | tf_op jit(solution)/shard_map/gradient/pallas_call | solution.py:344
  69.5 13.3 %backward.1 = (f32[128,16,128]{2,1,0:T(8,128)}, f32[1024,128]{1,0:T(8,128)}) custom-call(s32[16]{0:T(128)} %order.3, bf16[128,16,128]{2,1,0:T(8,128)(2,1)} %iq.3, bf16[128,16]{1,0:T(8,128)(2,1)} %copy.13.iw, bf16[4,2,16,1024]{3,2,1,0:T(8,128)(2,1)} %gradient.1.grad, bf16[1024,128]{1,0:T(8,128)(2,1)} %get-tuple-element.17.idx), custom_call_target="tpu_custom_call" | custom-call | tf_op jit(solution)/shard_map/backward/pallas_call | solution.py:424
  82.8 13.1 %reduce.1 = f32[32,128]{1,0:T(8,128)} custom-call(f32[8,128,128]{2,1,0:T(8,128)} %bitcast.4), custom_call_target="tpu_custom_call" | custom-call | tf_op jit(solution)/shard_map/reduce/pallas_call | solution.py:500
  95.9 1.3 %copy.15 = f32[32,128]{1,0:T(8,128)} copy(f32[32,128]{1,0:T(8,128)} %reduce.1) | data formatting | bytes 32768

commit v2 on v1

--- a/solution.py
+++ b/solution.py
@@ -49,7 +49,7 @@
     ctx, head = lax.axis_index("ctx"), lax.axis_index("head")
     group, core = ctx // 2, lax.rem(ctx, 2)
     sibling = group * 2 + 1 - core
-    rows = lat.shape[0]
+    rows = idx.shape[0]
     half = rows // 2
     share = half // shares
     own = [
@@ -59,7 +59,7 @@
     for e in range(2):
         take = pl.ds(pl.multiple_of(e * half + head * share, share), share)
         own.append(pltpu.make_async_copy(iq.at[take], iq_recv.at[head, e], local.at[2 + e]))
-        own.append(pltpu.make_async_copy(iw.at[take], iw_recv.at[head, e], local.at[4 + e]))
+    own.append(pltpu.make_async_copy(iw, iw_recv.at[head], local.at[4]))
     for copy in own:
         copy.start()
     enter(groups, shares)
@@ -78,12 +78,14 @@
         peer = lax.rem(head + step, shares)
         for e in range(2):
             take = pl.ds(pl.multiple_of(e * half + peer * share, share), share)
-            for src, dst, s, r in ((iq, iq_recv, qs, qr), (iw, iw_recv, ws, wr)):
-                copy = remote(
-                    src.at[take], dst.at[head, e], s.at[step, e], r.at[step, e], {"head": peer}
-                )
-                copy.start()
-                sent.append(copy)
+            copy = remote(
+                iq.at[take], iq_recv.at[head, e], qs.at[step, e], qr.at[step, e], {"head": peer}
+            )
+            copy.start()
+            sent.append(copy)
+        copy = remote(iw, iw_recv.at[head], ws.at[step], wr.at[step], {"head": peer})
+        copy.start()
+        sent.append(copy)
     for step in range(1, groups):
         source = lax.rem(group + groups - step, groups) * 2 + core
         for k, dst in enumerate((all_lat, all_idx)):
@@ -100,9 +102,10 @@
     for step in range(1, shares):
         source = lax.rem(head + shares - step, shares)
         for e in range(2):
-            for dst, s, r in ((iq_recv, qs, qr), (iw_recv, ws, wr)):
-                slot = dst.at[source, e]
-                remote(slot, slot, s.at[step, e], r.at[step, e], {"head": source}).wait_recv()
+            slot = iq_recv.at[source, e]
+            remote(slot, slot, qs.at[step, e], qr.at[step, e], {"head": source}).wait_recv()
+        slot = iw_recv.at[source]
+        remote(slot, slot, ws.at[step], wr.at[step], {"head": source}).wait_recv()
     for copy in sent:
         copy.wait_send()
     for copy in own:
@@ -111,7 +114,7 @@
 
 def gather(lat, idx, iq, iw, cycle, shares):
     groups = cycle // 2
-    rows = lat.shape[0]
+    rows = idx.shape[0]
     share = rows // 2 // shares
     dma = pltpu.SemaphoreType.DMA
     return pl.pallas_call(
@@ -120,13 +123,13 @@
             jax.ShapeDtypeStruct((cycle,) + lat.shape, lat.dtype),
             jax.ShapeDtypeStruct((cycle,) + idx.shape, idx.dtype),
             jax.ShapeDtypeStruct((shares, 2, share) + iq.shape[1:], iq.dtype),
-            jax.ShapeDtypeStruct((shares, 2, share) + iw.shape[1:], iw.dtype),
+            jax.ShapeDtypeStruct((shares,) + iw.shape, iw.dtype),
         ),
         in_specs=[pl.BlockSpec(memory_space=pl.ANY)] * 4,
         out_specs=[pl.BlockSpec(memory_space=pltpu.VMEM)] * 4,
         scratch_shapes=[
-            dma((6,)),
-            dma((shares, 2)), dma((shares, 2)), dma((shares, 2)), dma((shares, 2)),
+            dma((5,)),
+            dma((shares, 2)), dma((shares, 2)), dma((shares,)), dma((shares,)),
             dma((2, groups)), dma((2, groups)), dma((2, groups)), dma((2, groups)),
         ],
         compiler_params=pltpu.CompilerParams(collective_id=0, has_side_effects=True),
@@ -135,40 +138,46 @@
 
 
 def forward_kernel(
-    shares, tile, order, q, norm, lat, idx, iq, iw, sums, probs, idx_sorted, lat_sorted, logits
+    shares, tile, order, q, norm, lat, idx, iq, iw, sums, probs, idx_sorted, lat_sorted, logits, acc
 ):
     step, steps = pl.program_id(0), pl.num_programs(0)
     ctx, head = lax.axis_index("ctx"), lax.axis_index("head")
     blocks = order.shape[0]
-    half = lat.shape[0] // blocks
-    tokens = lat.shape[0]
+    tokens = idx.shape[0]
+    half = tokens // blocks
+    rows = 2 * half
     tiles = tokens // tile
     share = half // shares
-    heads = q.shape[1]
     idx_heads = iq.shape[3]
     idx_scale = (idx_heads * shares * iq.shape[4]) ** (-0.5)
 
     @pl.when(step == 0)
     def _():
-        def sort(r, carry):
-            src = pl.ds(pl.multiple_of(r * half, half), half)
-            dst = pl.ds(pl.multiple_of(order[r] * half, half), half)
-            lat_sorted[dst, :] = lat[src, :]
-            idx_sorted[dst, :] = idx[src, :]
+        acc[...] = jnp.zeros_like(acc)
+
+        def sort(c, carry):
+            pair = lat[c].T
+            for e in range(2):
+                src = pl.ds(pl.multiple_of((2 * c + e) * half, half), half)
+                dst = pl.ds(pl.multiple_of(order[2 * c + e] * half, half), half)
+                lat_sorted[dst, :] = pair[e * half : (e + 1) * half]
+                idx_sorted[dst, :] = idx[src, :]
             return carry
 
-        lax.fori_loop(0, blocks, sort, 0)
+        lax.fori_loop(0, blocks // 2, sort, 0)
         for e in range(2):
             block = order[2 * ctx + e]
             slot = (block >= blocks // 2).astype(jnp.int32)
             first = block * half + head * share
             logits[...] = jnp.full(logits.shape, -jnp.inf, jnp.float32)
-            weights = [
-                jnp.broadcast_to(
-                    (iw[z, e].astype(jnp.float32) * idx_scale)[:, :, None], (share, idx_heads, 128)
+            weights = []
+            for z in range(shares):
+                flat = iw[z].astype(jnp.float32).T * idx_scale
+                flat = sum(
+                    jnp.where(head == y, flat[e * half + y * share : e * half + (y + 1) * share], 0.0)
+                    for y in range(shares)
                 )
-                for z in range(shares)
-            ]
+                weights.append(jnp.broadcast_to(flat[:, :, None], (share, idx_heads, 128)))
 
             def logit_tile(k, carry):
                 cols = pl.ds(pl.multiple_of(k * tile, tile), tile)
@@ -198,53 +207,49 @@
             norm_sum = jnp.sum(expo, axis=1, keepdims=True)
             probs[pl.ds(pl.multiple_of(slot * share, share), share), :] = expo / norm_sum
 
-    chunk = q.shape[0]
-    per_block = half // chunk
-    e = step // per_block
-    inner = lax.rem(step, per_block)
-    block = order[2 * ctx + e]
-    slot = (block >= blocks // 2).astype(jnp.int32)
-    out_rows = pl.ds(pl.multiple_of(slot * half + inner * chunk, chunk), chunk)
-    first = block * half + inner * chunk
-    queries = q[...].reshape(chunk * heads, q.shape[2])
-    shift = jnp.broadcast_to((norm[...] * log2e)[:, :, None], (chunk, heads, 128))
-    count = (block * half + half - 1) // tile + 1
+    group = q.shape[0]
+    shift = norm[pl.ds(pl.multiple_of(step * group, group), group), :] * log2e
 
     def score_tile(k, carry):
-        cols = pl.ds(pl.multiple_of(k * tile, tile), tile)
-        scores = lax.dot_general(
-            queries, lat_sorted[cols, :], NT_DIMS, preferred_element_type=jnp.float32
-        ).reshape(chunk, heads, tile)
-        parts = [
-            jnp.sum(
-                jnp.exp2(scores[:, :, c : c + 128] * (mla_scale * log2e) - shift), axis=1
-            )
-            for c in range(0, tile, 128)
-        ]
-        total = jnp.concatenate(parts, axis=1)
-        shape = (chunk, tile)
-        visible = k * tile + lax.broadcasted_iota(
-            jnp.int32, shape, 1
-        ) <= first + lax.broadcasted_iota(jnp.int32, shape, 0)
-        sums[out_rows, cols] = jnp.where(visible, total, 0.0)
+        keys = lat_sorted[pl.ds(pl.multiple_of(k * tile, tile), tile), :]
+        total = acc[pl.ds(pl.multiple_of(k * tile, tile), tile), :]
+        for h in range(0, group, 2):
+            scores = jnp.dot(
+                keys, jnp.concatenate((q[h], q[h + 1]), axis=1), preferred_element_type=jnp.float32
+            ) * (mla_scale * log2e)
+            total = total + jnp.exp2(scores[:, :rows] - shift[h : h + 1])
+            total = total + jnp.exp2(scores[:, rows:] - shift[h + 1 : h + 2])
+        acc[pl.ds(pl.multiple_of(k * tile, tile), tile), :] = total
         return carry
 
-    lax.fori_loop(0, count, score_tile, 0)
-
-    def clear(k, carry):
-        cols = pl.ds(pl.multiple_of(k * tile, tile), tile)
-        sums[out_rows, cols] = jnp.zeros((chunk, tile), jnp.float32)
-        return carry
-
-    lax.fori_loop(count, tiles, clear, 0)
+    lax.fori_loop(0, tiles, score_tile, 0)
+
+    @pl.when(step == steps - 1)
+    def _():
+        def finish(k, carry):
+            cols = pl.ds(pl.multiple_of(k * tile, tile), tile)
+            total = acc[cols, :].T
+            shape = (half, tile)
+            for e in range(2):
+                block = order[2 * ctx + e]
+                slot = (block >= blocks // 2).astype(jnp.int32)
+                visible = k * tile + lax.broadcasted_iota(
+                    jnp.int32, shape, 1
+                ) <= block * half + lax.broadcasted_iota(jnp.int32, shape, 0)
+                sums[pl.ds(pl.multiple_of(slot * half, half), half), cols] = jnp.where(
+                    visible, total[e * half : (e + 1) * half], 0.0
+                )
+            return carry
+
+        lax.fori_loop(0, tiles, finish, 0)
 
 
 def forward(order, q, norm, lat, idx, iq, iw, shares):
-    rows, heads, width = q.shape
-    tokens = lat.shape[0]
+    heads, width, rows = q.shape
+    tokens = idx.shape[0]
     half = rows // 2
     share = half // shares
-    chunk = 16
+    group = 8
     tile = 256
     whole = lambda a: pl.BlockSpec(a.shape, lambda i, o: (0,) * a.ndim)
     return pl.pallas_call(
@@ -256,11 +261,10 @@
         ),
         grid_spec=pltpu.PrefetchScalarGridSpec(
             num_scalar_prefetch=1,
-            grid=(rows // chunk,),
+            grid=(heads // group,),
             in_specs=[
-                pl.BlockSpec((chunk, heads, width), lambda i, o: (i, 0, 0)),
-                pl.BlockSpec((chunk, heads), lambda i, o: (i, 0)),
-                whole(lat), whole(idx), whole(iq), whole(iw),
+                pl.BlockSpec((group, width, rows), lambda i, o: (i, 0, 0)),
+                whole(norm), whole(lat), whole(idx), whole(iq), whole(iw),
             ],
             out_specs=[
                 pl.BlockSpec((rows, tokens), lambda i, o: (0, 0)),
@@ -268,20 +272,22 @@
                 pl.BlockSpec(idx.shape, lambda i, o: (0, 0)),
             ],
             scratch_shapes=[
-                pltpu.VMEM(lat.shape, lat.dtype),
+                pltpu.VMEM((tokens, width), lat.dtype),
                 pltpu.VMEM((share, tokens), jnp.float32),
+                pltpu.VMEM((tokens, rows), jnp.float32),
             ],
         ),
         name="forward",
     )(order, q, norm, lat, idx, iq, iw)
 
 
-def gradient_kernel(shares, sums, probs, grad, low, high, ls, lr, hs, hr, gs, gr):
+def gradient_kernel(shares, sums, probs, grad, short_sums, low, high, ls, lr, hs, hr, gs, gr):
     head = lax.axis_index("head")
     rows, tokens = sums.shape
     half = rows // 2
     share = half // shares
     short = tokens // 2
+    short_sums[...] = sums[...].astype(jnp.bfloat16)
     enter(0, shares)
     sent = []
     for step in range(1, shares):
@@ -289,11 +295,11 @@
         start = pl.multiple_of(peer * share, share)
         for copy in (
             remote(
-                sums.at[pl.ds(start, share), pl.ds(0, short)], low.at[step], ls.at[step],
+                short_sums.at[pl.ds(start, share), pl.ds(0, short)], low.at[step], ls.at[step],
                 lr.at[step], {"head": peer},
             ),
             remote(
-                sums.at[pl.ds(half + start, share)], high.at[step], hs.at[step], hr.at[step],
+                short_sums.at[pl.ds(half + start, share)], high.at[step], hs.at[step], hr.at[step],
                 {"head": peer},
             ),
         ):
@@ -305,9 +311,9 @@
     for step in range(1, shares):
         source = lax.rem(head + shares - step, shares)
         remote(low.at[step], low.at[step], ls.at[step], lr.at[step], {"head": source}).wait_recv()
-        total_low = total_low + low[step]
+        total_low = total_low + low[step].astype(jnp.float32)
         remote(high.at[step], high.at[step], hs.at[step], hr.at[step], {"head": source}).wait_recv()
-        total_high = total_high + high[step]
+        total_high = total_high + high[step].astype(jnp.float32)
     row_low = jnp.sum(total_low, axis=1, keepdims=True)
     row_high = jnp.sum(total_high, axis=1, keepdims=True)
     grad[head, 0, :, :short] = (
@@ -347,8 +353,9 @@
         in_specs=[pl.BlockSpec(memory_space=pltpu.VMEM)] * 2,
         out_specs=pl.BlockSpec(memory_space=pltpu.VMEM),
         scratch_shapes=[
-            pltpu.VMEM((shares, share, tokens // 2), jnp.float32),
-            pltpu.VMEM((shares, share, tokens), jnp.float32),
+            pltpu.VMEM(sums.shape, jnp.bfloat16),
+            pltpu.VMEM((shares, share, tokens // 2), jnp.bfloat16),
+            pltpu.VMEM((shares, share, tokens), jnp.bfloat16),
             dma((shares,)), dma((shares,)), dma((shares,)), dma((shares,)),
             dma((2, shares)), dma((2, shares)),
         ],
@@ -357,7 +364,7 @@
     )(sums, probs)
 
 
-def backward_kernel(shares, tile, order, iq, iw, grad, idx, query_grad, key_grad, total):
+def backward_kernel(shares, tile, order, iq, iw, grad, idx, query_grad, key_grad, total, scaled):
     step, steps = pl.program_id(0), pl.num_programs(0)
     ctx = lax.axis_index("ctx")
     blocks = order.shape[0]
@@ -369,6 +376,7 @@
     @pl.when(step == 0)
     def _():
         total[...] = jnp.zeros_like(total)
+        scaled[...] = iw[...].astype(jnp.float32).T * idx_scale
 
     e = step // shares
     part = lax.rem(step, shares)
@@ -376,7 +384,7 @@
     slot = (block >= blocks // 2).astype(jnp.int32)
     queries = iq[...].reshape(share * heads, dim)
     weights = jnp.broadcast_to(
-        (iw[...].astype(jnp.float32) * idx_scale)[:, :, None], (share, heads, 128)
+        scaled[pl.ds(pl.multiple_of(step * share, share), share), :][:, :, None], (share, heads, 128)
     )
     query_grad[...] = jnp.zeros_like(query_grad)
 
@@ -432,7 +440,7 @@
             grid=(2 * shares,),
             in_specs=[
                 pl.BlockSpec((share, heads, dim), lambda i, o: (i, 0, 0)),
-                pl.BlockSpec((share, heads), lambda i, o: (i, 0)),
+                pl.BlockSpec(iw.shape, lambda i, o: (0, 0)),
                 pl.BlockSpec(grad.shape, lambda i, o: (0, 0, 0, 0)),
                 pl.BlockSpec(idx.shape, lambda i, o: (0, 0)),
             ],
@@ -440,7 +448,9 @@
                 pl.BlockSpec((share, heads, dim), lambda i, o: (i, 0, 0)),
                 pl.BlockSpec(idx.shape, lambda i, o: (0, 0)),
             ],
-            scratch_shapes=[pltpu.VMEM(idx.shape, jnp.float32)],
+            scratch_shapes=[
+                pltpu.VMEM(idx.shape, jnp.float32), pltpu.VMEM((rows, heads), jnp.float32)
+            ],
         ),
         name="backward",
     )(order, iq, iw, grad, idx)
@@ -517,17 +527,15 @@
     block_order, query_latent, key_latent, normalizer, indexer_query, indexer_key, indexer_weight
 ):
     cycle, shares = lax.axis_size("ctx"), lax.axis_size("head")
-    lat, idx, iq, iw = gather(
-        key_latent, indexer_key, indexer_query, indexer_weight, cycle, shares
-    )
-    lat = lat.reshape(-1, lat.shape[2])
+    weight = indexer_weight.T
+    lat, idx, iq, iw = gather(key_latent.T, indexer_key, indexer_query, weight, cycle, shares)
     idx = idx.reshape(-1, idx.shape[2])
     sums, probs, idx_sorted = forward(
-        block_order, query_latent, normalizer, lat, idx, iq, iw, shares
+        block_order, query_latent.transpose(1, 2, 0), normalizer.T, lat, idx, iq, iw, shares
     )
     grad = gradient(sums, probs, shares)
     query_grad, key_parts = backward(
-        block_order, indexer_query, indexer_weight, grad, idx_sorted, shares
+        block_order, indexer_query, weight, grad, idx_sorted, shares
     )
     return query_grad, reduce(key_parts, cycle, shares)
 

time: 97.5 us -> 79.7 us (0.82)
  local copies, waits for them, and re-layouts: 14.8 us -> 1.32 us
  Pallas kernels: 81.8 us -> 77.3 us
    unnamed x5 -> x1, local copies, waits for them, and re-layouts: 14.8 us -> 1.32 us
    pallas_call x1, Pallas kernels: 19 us -> 15.1 us  [gradient(): pl.pallas_call(functools.partial(gradient_kernel, shares), out_shape=jax....]
where the time goes in v2:
time: 79.7 us; the launch traced here: 79.2 us
  Pallas kernels  77.3 us (97%)
  local copies, waits for them, and re-layouts  1.32 us (2%)
    pallas_call x1, Pallas kernels, gather(): pl.pallas_call(functools.partial(gather_kernel, groups, shares), out_shap...  18.9 us
    pallas_call x1, Pallas kernels, forward(): pl.pallas_call(functools.partial(forward_kernel, shares, tile), out_shape...  17 us
    pallas_call x1, Pallas kernels, gradient(): pl.pallas_call(functools.partial(gradient_kernel, shares), out_shape=jax....  15.1 us
    pallas_call x1, Pallas kernels, reduce(): pl.pallas_call(functools.partial(reduce_kernel, groups, shares), out_shap...  13.4 us
    pallas_call x1, Pallas kernels, backward(): pl.pallas_call(functools.partial(backward_kernel, shares, tile), out_shap...  12.8 us

profile of v2, /device:TPU:0, one launch (start us, length us, event | category | flops | bytes accessed | tf_op | source)
XLA Modules:
  0.0 79.2 jit_solution(17407143820328731080)
XLA Ops:
  0.6 18.9 %gather.1 = (bf16[8,576,128]{2,1,0:T(8,128)(2,1)}, bf16[8,128,128]{2,1,0:T(8,128)(2,1)}, bf16[4,2,16,16,128]{4,3,2,1,0:T(8,128)(2,1)}, bf16[4,16,128]{2,1,0:T(8,128)(2,1)}) custom-call(bf16[576,128]{1,0:T(8,128)(2,1)} %bitcast.9, bf16[128,128]{1,0:T(8,128)(2,1)} %idx.1, bf16[128,16,128]{2,1,0:T(8,128)(2,1)} %iq.3, bf16[16,128]{1,0:T(8,128)(2,1)} %bitcast.11), custom_call_target="tpu_custom_call" | custom-call | tf_op jit(solution)/shard_map/gather/pallas_call | solution.py:120
  19.5 17.0 %forward.1 = (f32[128,1024]{1,0:T(8,128)}, f32[32,1024]{1,0:T(8,128)}, bf16[1024,128]{1,0:T(8,128)(2,1)}) custom-call(s32[16]{0:T(128)} %order.3, bf16[32,576,128]{2,1,0:T(8,128)(2,1)} %bitcast.6, f32[32,128]{1,0:T(8,128)} %bitcast.10, bf16[8,576,128]{2,1,0:T(8,128)(2,1)} %get-tuple-element.11.lat, bf16[1024,128]{1,0:T(8,128)(2,1)} %bitcast.8, ...), custom_call_target="tpu_custom_call" | custom-call | tf_op jit(solution)/shard_map/forward/pallas_call | solution.py:255
  36.5 15.1 %gradient.1.grad = bf16[4,2,16,1024]{3,2,1,0:T(8,128)(2,1)} custom-call(f32[128,1024]{1,0:T(8,128)} %get-tuple-element.15.sums, f32[32,1024]{1,0:T(8,128)} %get-tuple-element.16.probs), custom_call_target="tpu_custom_call" | custom-call | tf_op jit(solution)/shard_map/gradient/pallas_call | solution.py:350
  51.7 12.8 %backward.1 = (f32[128,16,128]{2,1,0:T(8,128)}, f32[1024,128]{1,0:T(8,128)}) custom-call(s32[16]{0:T(128)} %order.3, bf16[128,16,128]{2,1,0:T(8,128)(2,1)} %iq.3, bf16[16,128]{1,0:T(8,128)(2,1)} %bitcast.12, bf16[4,2,16,1024]{3,2,1,0:T(8,128)(2,1)} %gradient.1.grad, bf16[1024,128]{1,0:T(8,128)(2,1)} %get-tuple-element.17.idx), custom_call_target="tpu_custom_call" | custom-call | tf_op jit(solution)/shard_map/backward/pallas_call | solution.py:432
  64.5 13.4 %reduce.1 = f32[32,128]{1,0:T(8,128)} custom-call(f32[8,128,128]{2,1,0:T(8,128)} %bitcast.7), custom_call_target="tpu_custom_call" | custom-call | tf_op jit(solution)/shard_map/reduce/pallas_call | solution.py:510
  77.9 1.3 %copy.10 = f32[32,128]{1,0:T(8,128)} copy(f32[32,128]{1,0:T(8,128)} %reduce.1) | data formatting | bytes 32768

commit v3 on v2

--- a/solution.py
+++ b/solution.py
@@ -43,8 +43,8 @@
 
 
 def gather_kernel(
-    groups, shares, lat, idx, iq, iw, all_lat, all_idx, iq_recv, iw_recv,
-    local, qs, qr, ws, wr, ds, dr, fs, fr,
+    groups, shares, lat, idx, iq, iw, q_far, norm, acc, all_idx, iq_recv, iw_recv,
+    all_lat, q, keys, local, qs, qr, ws, wr, ds, dr, fs, fr,
 ):
     ctx, head = lax.axis_index("ctx"), lax.axis_index("head")
     group, core = ctx // 2, lax.rem(ctx, 2)
@@ -60,8 +60,29 @@
         take = pl.ds(pl.multiple_of(e * half + head * share, share), share)
         own.append(pltpu.make_async_copy(iq.at[take], iq_recv.at[head, e], local.at[2 + e]))
     own.append(pltpu.make_async_copy(iw, iw_recv.at[head], local.at[4]))
+    own.append(pltpu.make_async_copy(q_far, q, local.at[5]))
     for copy in own:
         copy.start()
+    heads, bundle = q.shape[0], 8
+
+    def score(source):
+        keys[...] = jnp.concatenate((all_lat[2 * source], all_lat[2 * source + 1]), axis=1).T
+
+        def body(i, total):
+            shift = norm[pl.ds(pl.multiple_of(i * bundle, bundle), bundle), :] * log2e
+            for h in range(0, bundle, 2):
+                pair = jnp.concatenate((q[i * bundle + h], q[i * bundle + h + 1]), axis=1)
+                scores = jnp.dot(keys[...], pair, preferred_element_type=jnp.float32) * (
+                    mla_scale * log2e
+                )
+                total = total + jnp.exp2(scores[:, :rows] - shift[h : h + 1])
+                total = total + jnp.exp2(scores[:, rows:] - shift[h + 1 : h + 2])
+            return total
+
+        acc[source] = lax.fori_loop(
+            0, heads // bundle, body, jnp.zeros((2 * rows, rows), jnp.float32)
+        )
+
     enter(groups, shares)
     sent = []
     for step in range(1, groups):
@@ -86,6 +107,11 @@
         copy = remote(iw, iw_recv.at[head], ws.at[step], wr.at[step], {"head": peer})
         copy.start()
         sent.append(copy)
+    slot = all_lat.at[sibling]
+    remote(slot, slot, fs.at[0, 0], fr.at[0, 0], {"ctx": sibling}).wait_recv()
+    own[0].wait()
+    own[-1].wait()
+    score(group)
     for step in range(1, groups):
         source = lax.rem(group + groups - step, groups) * 2 + core
         for k, dst in enumerate((all_lat, all_idx)):
@@ -94,11 +120,14 @@
             copy = remote(slot, slot, fs.at[k, step], fr.at[k, step], {"ctx": sibling})
             copy.start()
             sent.append(copy)
-    for step in range(groups):
-        source = lax.rem(group + groups - step, groups) * 2 + 1 - core
+    slot = all_idx.at[sibling]
+    remote(slot, slot, fs.at[1, 0], fr.at[1, 0], {"ctx": sibling}).wait_recv()
+    for step in range(1, groups):
+        source = lax.rem(group + groups - step, groups)
         for k, dst in enumerate((all_lat, all_idx)):
-            slot = dst.at[source]
+            slot = dst.at[source * 2 + 1 - core]
             remote(slot, slot, fs.at[k, step], fr.at[k, step], {"ctx": sibling}).wait_recv()
+        score(source)
     for step in range(1, shares):
         source = lax.rem(head + shares - step, shares)
         for e in range(2):
@@ -108,11 +137,11 @@
         remote(slot, slot, ws.at[step], wr.at[step], {"head": source}).wait_recv()
     for copy in sent:
         copy.wait_send()
-    for copy in own:
+    for copy in own[1:-1]:
         copy.wait()
 
 
-def gather(lat, idx, iq, iw, cycle, shares):
+def gather(lat, idx, iq, iw, q, norm, cycle, shares):
     groups = cycle // 2
     rows = idx.shape[0]
     share = rows // 2 // shares
@@ -120,27 +149,30 @@
     return pl.pallas_call(
         functools.partial(gather_kernel, groups, shares),
         out_shape=(
-            jax.ShapeDtypeStruct((cycle,) + lat.shape, lat.dtype),
+            jax.ShapeDtypeStruct((groups, 2 * rows, rows), jnp.float32),
             jax.ShapeDtypeStruct((cycle,) + idx.shape, idx.dtype),
             jax.ShapeDtypeStruct((shares, 2, share) + iq.shape[1:], iq.dtype),
             jax.ShapeDtypeStruct((shares,) + iw.shape, iw.dtype),
         ),
-        in_specs=[pl.BlockSpec(memory_space=pl.ANY)] * 4,
+        in_specs=[pl.BlockSpec(memory_space=pl.ANY)] * 5
+        + [pl.BlockSpec(memory_space=pltpu.VMEM)],
         out_specs=[pl.BlockSpec(memory_space=pltpu.VMEM)] * 4,
         scratch_shapes=[
-            dma((5,)),
+            pltpu.VMEM((cycle,) + lat.shape, lat.dtype),
+            pltpu.VMEM(q.shape, q.dtype),
+            pltpu.VMEM((2 * rows, lat.shape[0]), lat.dtype),
+            dma((6,)),
             dma((shares, 2)), dma((shares, 2)), dma((shares,)), dma((shares,)),
             dma((2, groups)), dma((2, groups)), dma((2, groups)), dma((2, groups)),
         ],
         compiler_params=pltpu.CompilerParams(collective_id=0, has_side_effects=True),
         name="gather",
-    )(lat, idx, iq, iw)
+    )(lat, idx, iq, iw, q, norm)
 
 
 def forward_kernel(
-    shares, tile, order, q, norm, lat, idx, iq, iw, sums, probs, idx_sorted, lat_sorted, logits, acc
+    shares, tile, order, lat, idx, iq, iw, sums, probs, idx_sorted, logits, acc
 ):
-    step, steps = pl.program_id(0), pl.num_programs(0)
     ctx, head = lax.axis_index("ctx"), lax.axis_index("head")
     blocks = order.shape[0]
     tokens = idx.shape[0]
@@ -151,134 +183,94 @@
     idx_heads = iq.shape[3]
     idx_scale = (idx_heads * shares * iq.shape[4]) ** (-0.5)
 
-    @pl.when(step == 0)
-    def _():
-        acc[...] = jnp.zeros_like(acc)
-
-        def sort(c, carry):
-            pair = lat[c].T
-            for e in range(2):
-                src = pl.ds(pl.multiple_of((2 * c + e) * half, half), half)
-                dst = pl.ds(pl.multiple_of(order[2 * c + e] * half, half), half)
-                lat_sorted[dst, :] = pair[e * half : (e + 1) * half]
-                idx_sorted[dst, :] = idx[src, :]
+    def sort(c, carry):
+        for e in range(2):
+            src = pl.ds(pl.multiple_of((2 * c + e) * half, half), half)
+            dst = pl.ds(pl.multiple_of(order[2 * c + e] * half, half), half)
+            acc[dst, :] = lat[src, :]
+            idx_sorted[dst, :] = idx[src, :]
+        return carry
+
+    lax.fori_loop(0, blocks // 2, sort, 0)
+    for e in range(2):
+        block = order[2 * ctx + e]
+        slot = (block >= blocks // 2).astype(jnp.int32)
+        first = block * half + head * share
+        logits[...] = jnp.full(logits.shape, -jnp.inf, jnp.float32)
+        weights = []
+        for z in range(shares):
+            flat = iw[z].astype(jnp.float32).T * idx_scale
+            flat = sum(
+                jnp.where(head == y, flat[e * half + y * share : e * half + (y + 1) * share], 0.0)
+                for y in range(shares)
+            )
+            weights.append(jnp.broadcast_to(flat[:, :, None], (share, idx_heads, 128)))
+
+        def logit_tile(k, carry):
+            cols = pl.ds(pl.multiple_of(k * tile, tile), tile)
+            keys = idx_sorted[cols, :]
+            total = jnp.zeros((share, tile), jnp.float32)
+            for z in range(shares):
+                dots = lax.dot_general(
+                    iq[z, e].reshape(share * idx_heads, -1), keys, NT_DIMS,
+                    preferred_element_type=jnp.float32,
+                ).reshape(share, idx_heads, tile)
+                parts = [
+                    jnp.sum(weights[z] * jnp.maximum(dots[:, :, c : c + 128], 0.0), axis=1)
+                    for c in range(0, tile, 128)
+                ]
+                total = total + jnp.concatenate(parts, axis=1)
+            shape = (share, tile)
+            visible = k * tile + lax.broadcasted_iota(
+                jnp.int32, shape, 1
+            ) <= first + lax.broadcasted_iota(jnp.int32, shape, 0)
+            logits[:, cols] = jnp.where(visible, total, -jnp.inf)
             return carry
 
-        lax.fori_loop(0, blocks // 2, sort, 0)
+        lax.fori_loop(0, (block * half + half - 1) // tile + 1, logit_tile, 0)
+        values = logits[...]
+        top = jnp.max(values, axis=1, keepdims=True)
+        expo = jnp.exp(values - top)
+        norm_sum = jnp.sum(expo, axis=1, keepdims=True)
+        probs[pl.ds(pl.multiple_of(slot * share, share), share), :] = expo / norm_sum
+
+    def finish(k, carry):
+        cols = pl.ds(pl.multiple_of(k * tile, tile), tile)
+        total = acc[cols, :].T
+        shape = (half, tile)
         for e in range(2):
             block = order[2 * ctx + e]
             slot = (block >= blocks // 2).astype(jnp.int32)
-            first = block * half + head * share
-            logits[...] = jnp.full(logits.shape, -jnp.inf, jnp.float32)
-            weights = []
-            for z in range(shares):
-                flat = iw[z].astype(jnp.float32).T * idx_scale
-                flat = sum(
-                    jnp.where(head == y, flat[e * half + y * share : e * half + (y + 1) * share], 0.0)
-                    for y in range(shares)
-                )
-                weights.append(jnp.broadcast_to(flat[:, :, None], (share, idx_heads, 128)))
-
-            def logit_tile(k, carry):
-                cols = pl.ds(pl.multiple_of(k * tile, tile), tile)
-                keys = idx_sorted[cols, :]
-                total = jnp.zeros((share, tile), jnp.float32)
-                for z in range(shares):
-                    dots = lax.dot_general(
-                        iq[z, e].reshape(share * idx_heads, -1), keys, NT_DIMS,
-                        preferred_element_type=jnp.float32,
-                    ).reshape(share, idx_heads, tile)
-                    parts = [
-                        jnp.sum(weights[z] * jnp.maximum(dots[:, :, c : c + 128], 0.0), axis=1)
-                        for c in range(0, tile, 128)
-                    ]
-                    total = total + jnp.concatenate(parts, axis=1)
-                shape = (share, tile)
-                visible = k * tile + lax.broadcasted_iota(
-                    jnp.int32, shape, 1
-                ) <= first + lax.broadcasted_iota(jnp.int32, shape, 0)
-                logits[:, cols] = jnp.where(visible, total, -jnp.inf)
-                return carry
-
-            lax.fori_loop(0, (block * half + half - 1) // tile + 1, logit_tile, 0)
-            values = logits[...]
-            top = jnp.max(values, axis=1, keepdims=True)
-            expo = jnp.exp(values - top)
-            norm_sum = jnp.sum(expo, axis=1, keepdims=True)
-            probs[pl.ds(pl.multiple_of(slot * share, share), share), :] = expo / norm_sum
-
-    group = q.shape[0]
-    shift = norm[pl.ds(pl.multiple_of(step * group, group), group), :] * log2e
-
-    def score_tile(k, carry):
-        keys = lat_sorted[pl.ds(pl.multiple_of(k * tile, tile), tile), :]
-        total = acc[pl.ds(pl.multiple_of(k * tile, tile), tile), :]
-        for h in range(0, group, 2):
-            scores = jnp.dot(
-                keys, jnp.concatenate((q[h], q[h + 1]), axis=1), preferred_element_type=jnp.float32
-            ) * (mla_scale * log2e)
-            total = total + jnp.exp2(scores[:, :rows] - shift[h : h + 1])
-            total = total + jnp.exp2(scores[:, rows:] - shift[h + 1 : h + 2])
-        acc[pl.ds(pl.multiple_of(k * tile, tile), tile), :] = total
+            visible = k * tile + lax.broadcasted_iota(
+                jnp.int32, shape, 1
+            ) <= block * half + lax.broadcasted_iota(jnp.int32, shape, 0)
+            sums[pl.ds(pl.multiple_of(slot * half, half), half), cols] = jnp.where(
+                visible, total[e * half : (e + 1) * half], 0.0
+            )
         return carry
 
-    lax.fori_loop(0, tiles, score_tile, 0)
-
-    @pl.when(step == steps - 1)
-    def _():
-        def finish(k, carry):
-            cols = pl.ds(pl.multiple_of(k * tile, tile), tile)
-            total = acc[cols, :].T
-            shape = (half, tile)
-            for e in range(2):
-                block = order[2 * ctx + e]
-                slot = (block >= blocks // 2).astype(jnp.int32)
-                visible = k * tile + lax.broadcasted_iota(
-                    jnp.int32, shape, 1
-                ) <= block * half + lax.broadcasted_iota(jnp.int32, shape, 0)
-                sums[pl.ds(pl.multiple_of(slot * half, half), half), cols] = jnp.where(
-                    visible, total[e * half : (e + 1) * half], 0.0
-                )
-            return carry
-
-        lax.fori_loop(0, tiles, finish, 0)
-
-
-def forward(order, q, norm, lat, idx, iq, iw, shares):
-    heads, width, rows = q.shape
-    tokens = idx.shape[0]
-    half = rows // 2
-    share = half // shares
-    group = 8
-    tile = 256
-    whole = lambda a: pl.BlockSpec(a.shape, lambda i, o: (0,) * a.ndim)
+    lax.fori_loop(0, tiles, finish, 0)
+
+
+def forward(order, lat, idx, iq, iw, shares):
+    tokens, rows = lat.shape
+    share = rows // 2 // shares
+    vmem = pl.BlockSpec(memory_space=pltpu.VMEM)
     return pl.pallas_call(
-        functools.partial(forward_kernel, shares, tile),
+        functools.partial(forward_kernel, shares, 256),
         out_shape=(
             jax.ShapeDtypeStruct((rows, tokens), jnp.float32),
             jax.ShapeDtypeStruct((2 * share, tokens), jnp.float32),
             jax.ShapeDtypeStruct(idx.shape, idx.dtype),
         ),
-        grid_spec=pltpu.PrefetchScalarGridSpec(
-            num_scalar_prefetch=1,
-            grid=(heads // group,),
-            in_specs=[
-                pl.BlockSpec((group, width, rows), lambda i, o: (i, 0, 0)),
-                whole(norm), whole(lat), whole(idx), whole(iq), whole(iw),
-            ],
-            out_specs=[
-                pl.BlockSpec((rows, tokens), lambda i, o: (0, 0)),
-                pl.BlockSpec((2 * share, tokens), lambda i, o: (0, 0)),
-                pl.BlockSpec(idx.shape, lambda i, o: (0, 0)),
-            ],
-            scratch_shapes=[
-                pltpu.VMEM((tokens, width), lat.dtype),
-                pltpu.VMEM((share, tokens), jnp.float32),
-                pltpu.VMEM((tokens, rows), jnp.float32),
-            ],
-        ),
+        in_specs=[pl.BlockSpec(memory_space=pltpu.SMEM)] + [vmem] * 4,
+        out_specs=[vmem] * 3,
+        scratch_shapes=[
+            pltpu.VMEM((share, tokens), jnp.float32),
+            pltpu.VMEM((tokens, rows), jnp.float32),
+        ],
         name="forward",
-    )(order, q, norm, lat, idx, iq, iw)
+    )(order, lat, idx, iq, iw)
 
 
 def gradient_kernel(shares, sums, probs, grad, short_sums, low, high, ls, lr, hs, hr, gs, gr):
@@ -528,10 +520,13 @@
 ):
     cycle, shares = lax.axis_size("ctx"), lax.axis_size("head")
     weight = indexer_weight.T
-    lat, idx, iq, iw = gather(key_latent.T, indexer_key, indexer_query, weight, cycle, shares)
+    partial, idx, iq, iw = gather(
+        key_latent.T, indexer_key, indexer_query, weight, query_latent.transpose(1, 2, 0),
+        normalizer.T, cycle, shares,
+    )
     idx = idx.reshape(-1, idx.shape[2])
     sums, probs, idx_sorted = forward(
-        block_order, query_latent.transpose(1, 2, 0), normalizer.T, lat, idx, iq, iw, shares
+        block_order, partial.reshape(-1, partial.shape[2]), idx, iq, iw, shares
     )
     grad = gradient(sums, probs, shares)
     query_grad, key_parts = backward(

time: 79.7 us -> 72 us (0.903)
  Pallas kernels: 77.3 us -> 69.5 us
    pallas_call x1, Pallas kernels: 17 us -> 5.41 us  [forward(): pl.pallas_call(functools.partial(forward_kernel, shares, 256), out_shape=...]
    pallas_call x1, Pallas kernels: 18.9 us -> 24.9 us  [gather(): pl.pallas_call(functools.partial(gather_kernel, groups, shares), out_shap...]
    pallas_call x1, Pallas kernels: 15.1 us -> 13.5 us  [gradient(): pl.pallas_call(functools.partial(gradient_kernel, shares), out_shape=jax....]
where the time goes in v3:
time: 72 us; the launch traced here: 71.5 us
  Pallas kernels  69.5 us (97%)
  local copies, waits for them, and re-layouts  1.32 us (2%)
    pallas_call x1, Pallas kernels, gather(): pl.pallas_call(functools.partial(gather_kernel, groups, shares), out_shap...  24.9 us
    pallas_call x1, Pallas kernels, gradient(): pl.pallas_call(functools.partial(gradient_kernel, shares), out_shape=jax....  13.5 us
    pallas_call x1, Pallas kernels, backward(): pl.pallas_call(functools.partial(backward_kernel, shares, tile), out_shap...  12.8 us
    pallas_call x1, Pallas kernels, reduce(): pl.pallas_call(functools.partial(reduce_kernel, groups, shares), out_shap...  12.8 us
    pallas_call x1, Pallas kernels, forward(): pl.pallas_call(functools.partial(forward_kernel, shares, 256), out_shape=...  5.41 us

profile of v3, /device:TPU:0, one launch (start us, length us, event | category | flops | bytes accessed | tf_op | source)
XLA Modules:
  0.0 71.5 jit_solution(153118262412658442)
XLA Ops:
  0.6 24.9 %gather.1 = (f32[4,256,128]{2,1,0:T(8,128)}, bf16[8,128,128]{2,1,0:T(8,128)(2,1)}, bf16[4,2,16,16,128]{4,3,2,1,0:T(8,128)(2,1)}, bf16[4,16,128]{2,1,0:T(8,128)(2,1)}) custom-call(bf16[576,128]{1,0:T(8,128)(2,1)} %bitcast.11, bf16[128,128]{1,0:T(8,128)(2,1)} %idx.1, bf16[128,16,128]{2,1,0:T(8,128)(2,1)} %iq.3, bf16[16,128]{1,0:T(8,128)(2,1)} %bitcast.13, ...), custom_call_target="tpu_custom_call" | custom-call | tf_op jit(solution)/shard_map/gather/pallas_call | solution.py:149
  25.6 5.4 %forward.1 = (f32[128,1024]{1,0:T(8,128)}, f32[32,1024]{1,0:T(8,128)}, bf16[1024,128]{1,0:T(8,128)(2,1)}) custom-call(s32[16]{0:T(128)} %order.3, f32[1024,128]{1,0:T(8,128)} %bitcast.8, bf16[1024,128]{1,0:T(8,128)(2,1)} %bitcast.10, bf16[4,2,16,16,128]{4,3,2,1,0:T(8,128)(2,1)} %get-tuple-element.13.iq, bf16[4,16,128]{2,1,0:T(8,128)(2,1)} %get-tuple-element.14.iw), custom_call_target="tpu_custom_call" | custom-call | tf_op jit(solution)/shard_map/forward/pallas_call | solution.py:259
  31.0 13.5 %gradient.1.grad = bf16[4,2,16,1024]{3,2,1,0:T(8,128)(2,1)} custom-call(f32[128,1024]{1,0:T(8,128)} %get-tuple-element.15.sums, f32[32,1024]{1,0:T(8,128)} %get-tuple-element.16.probs), custom_call_target="tpu_custom_call" | custom-call | tf_op jit(solution)/shard_map/gradient/pallas_call | solution.py:342
  44.5 12.8 %backward.1 = (f32[128,16,128]{2,1,0:T(8,128)}, f32[1024,128]{1,0:T(8,128)}) custom-call(s32[16]{0:T(128)} %order.3, bf16[128,16,128]{2,1,0:T(8,128)(2,1)} %iq.3, bf16[16,128]{1,0:T(8,128)(2,1)} %bitcast.14, bf16[4,2,16,1024]{3,2,1,0:T(8,128)(2,1)} %gradient.1.grad, bf16[1024,128]{1,0:T(8,128)(2,1)} %get-tuple-element.17.idx), custom_call_target="tpu_custom_call" | custom-call | tf_op jit(solution)/shard_map/backward/pallas_call | solution.py:424
  57.3 12.8 %reduce.1 = f32[32,128]{1,0:T(8,128)} custom-call(f32[8,128,128]{2,1,0:T(8,128)} %bitcast.9), custom_call_target="tpu_custom_call" | custom-call | tf_op jit(solution)/shard_map/reduce/pallas_call | solution.py:502
  70.2 1.3 %copy.10 = f32[32,128]{1,0:T(8,128)} copy(f32[32,128]{1,0:T(8,128)} %reduce.1) | data formatting | bytes 32768

commit v4 on v3

--- a/solution.py
+++ b/solution.py
@@ -40,6 +40,15 @@
     return pltpu.make_async_remote_copy(
         src_ref=src, dst_ref=dst, send_sem=send, recv_sem=recv, device_id=device, device_id_type=MESH
     )
+
+
+def partner(group, step, groups):
+    bit = 1
+    while bit < groups:
+        if step & bit:
+            group = group + bit * (1 - 2 * lax.rem(group // bit, 2))
+        bit *= 2
+    return group
 
 
 def gather_kernel(
@@ -86,7 +95,7 @@
     enter(groups, shares)
     sent = []
     for step in range(1, groups):
-        peer = lax.rem(group + step, groups) * 2 + core
+        peer = partner(group, step, groups) * 2 + core
         for k, (src, dst) in enumerate(((lat, all_lat), (idx, all_idx))):
             copy = remote(src, dst.at[ctx], ds.at[k, step], dr.at[k, step], {"ctx": peer})
             copy.start()
@@ -112,22 +121,30 @@
     own[0].wait()
     own[-1].wait()
     score(group)
-    for step in range(1, groups):
-        source = lax.rem(group + groups - step, groups) * 2 + core
+    slot = all_idx.at[sibling]
+    remote(slot, slot, fs.at[1, 0], fr.at[1, 0], {"ctx": sibling}).wait_recv()
+
+    def relay(step):
+        source = partner(group, step, groups) * 2 + core
         for k, dst in enumerate((all_lat, all_idx)):
             slot = dst.at[source]
             remote(slot, slot, ds.at[k, step], dr.at[k, step], {"ctx": sibling}).wait_recv()
             copy = remote(slot, slot, fs.at[k, step], fr.at[k, step], {"ctx": sibling})
             copy.start()
             sent.append(copy)
-    slot = all_idx.at[sibling]
-    remote(slot, slot, fs.at[1, 0], fr.at[1, 0], {"ctx": sibling}).wait_recv()
-    for step in range(1, groups):
-        source = lax.rem(group + groups - step, groups)
+
+    def consume(step):
+        source = partner(group, step, groups)
         for k, dst in enumerate((all_lat, all_idx)):
             slot = dst.at[source * 2 + 1 - core]
             remote(slot, slot, fs.at[k, step], fr.at[k, step], {"ctx": sibling}).wait_recv()
         score(source)
+
+    for step in range(1, groups + 1):
+        if step < groups:
+            relay(step)
+        if 0 < step - 1 < groups:
+            consume(step - 1)
     for step in range(1, shares):
         source = lax.rem(head + shares - step, shares)
         for e in range(2):
@@ -257,7 +274,7 @@
     share = rows // 2 // shares
     vmem = pl.BlockSpec(memory_space=pltpu.VMEM)
     return pl.pallas_call(
-        functools.partial(forward_kernel, shares, 256),
+        functools.partial(forward_kernel, shares, math.gcd(tokens // 2, 512)),
         out_shape=(
             jax.ShapeDtypeStruct((rows, tokens), jnp.float32),
             jax.ShapeDtypeStruct((2 * share, tokens), jnp.float32),
@@ -362,7 +379,9 @@
     blocks = order.shape[0]
     tokens = idx.shape[0]
     half = tokens // blocks
-    share, heads, dim = iq.shape
+    count, heads, dim = iq.shape
+    share = grad.shape[2]
+    parts_each = count // share
     idx_scale = (heads * shares * dim) ** (-0.5)
 
     @pl.when(step == 0)
@@ -370,13 +389,13 @@
         total[...] = jnp.zeros_like(total)
         scaled[...] = iw[...].astype(jnp.float32).T * idx_scale
 
-    e = step // shares
-    part = lax.rem(step, shares)
+    e = step // (steps // 2)
+    part = pl.ds(lax.rem(step, steps // 2) * parts_each, parts_each)
     block = order[2 * ctx + e]
     slot = (block >= blocks // 2).astype(jnp.int32)
-    queries = iq[...].reshape(share * heads, dim)
+    queries = iq[...].reshape(count * heads, dim)
     weights = jnp.broadcast_to(
-        scaled[pl.ds(pl.multiple_of(step * share, share), share), :][:, :, None], (share, heads, 128)
+        scaled[pl.ds(pl.multiple_of(step * count, count), count), :][:, :, None], (count, heads, 128)
     )
     query_grad[...] = jnp.zeros_like(query_grad)
 
@@ -385,8 +404,8 @@
         keys = idx[cols, :]
         dots = lax.dot_general(
             queries, keys, NT_DIMS, preferred_element_type=jnp.float32
-        ).reshape(share, heads, tile)
-        rate = grad[part, slot, :, cols].astype(jnp.float32)
+        ).reshape(count, heads, tile)
+        rate = grad[part, slot, :, cols].reshape(count, tile).astype(jnp.float32)
         parts = [
             jnp.where(
                 dots[:, :, c : c + 128] > 0, rate[:, None, c : c + 128] * weights, 0.0
@@ -394,11 +413,11 @@
             for c in range(0, tile, 128)
         ]
         coefficient = (
-            jnp.concatenate(parts, axis=2).reshape(share * heads, tile).astype(jnp.bfloat16)
+            jnp.concatenate(parts, axis=2).reshape(count * heads, tile).astype(jnp.bfloat16)
         )
         query_grad[...] += jnp.dot(
             coefficient, keys, preferred_element_type=jnp.float32
-        ).reshape(share, heads, dim)
+        ).reshape(count, heads, dim)
         total[cols, :] += lax.dot_general(
             coefficient, queries, TN_DIMS, preferred_element_type=jnp.float32
         )
@@ -420,7 +439,8 @@
 def backward(order, iq, iw, grad, idx, shares):
     rows, heads, dim = iq.shape
     share = rows // 2 // shares
-    tile = 256
+    count = share * shares
+    tile = math.gcd(idx.shape[0] // 2, 512)
     return pl.pallas_call(
         functools.partial(backward_kernel, shares, tile),
         out_shape=(
@@ -429,15 +449,15 @@
         ),
         grid_spec=pltpu.PrefetchScalarGridSpec(
             num_scalar_prefetch=1,
-            grid=(2 * shares,),
+            grid=(rows // count,),
             in_specs=[
-                pl.BlockSpec((share, heads, dim), lambda i, o: (i, 0, 0)),
+                pl.BlockSpec((count, heads, dim), lambda i, o: (i, 0, 0)),
                 pl.BlockSpec(iw.shape, lambda i, o: (0, 0)),
                 pl.BlockSpec(grad.shape, lambda i, o: (0, 0, 0, 0)),
                 pl.BlockSpec(idx.shape, lambda i, o: (0, 0)),
             ],
             out_specs=[
-                pl.BlockSpec((share, heads, dim), lambda i, o: (i, 0, 0)),
+                pl.BlockSpec((count, heads, dim), lambda i, o: (i, 0, 0)),
                 pl.BlockSpec(idx.shape, lambda i, o: (0, 0)),
             ],
             scratch_shapes=[
@@ -465,7 +485,7 @@
     for step in range(1, groups):
         peer = lax.rem(group + step, groups)
         remote(near.at[step], near.at[step], ns.at[step], nr.at[step], {"ctx": sibling}).wait_recv()
-        acc[step] = parts[peer * 2 + core] + near[step]
+        acc[step] = (parts[peer * 2 + core] + near[step]).astype(jnp.bfloat16)
         copy = remote(
             acc.at[step], mid.at[step], ms.at[step], mr.at[step], {"ctx": peer * 2 + core}
         )
@@ -475,7 +495,7 @@
     value = parts[ctx] + near[0]
     for step in range(1, groups):
         remote(mid.at[step], mid.at[step], ms.at[step], mr.at[step], {"ctx": sibling}).wait_recv()
-        value = value + mid[step]
+        value = value + mid[step].astype(jnp.float32)
     last[...] = value
     for step in range(1, shares):
         peer = lax.rem(head + step, shares)
@@ -498,14 +518,15 @@
     groups = cycle // 2
     rows, dim = parts.shape[0] // cycle, parts.shape[1]
     dma = pltpu.SemaphoreType.DMA
-    buffer = pltpu.VMEM((groups, rows, dim), jnp.float32)
+    buffer = pltpu.VMEM((groups, rows, dim), jnp.bfloat16)
     return pl.pallas_call(
         functools.partial(reduce_kernel, groups, shares),
         out_shape=jax.ShapeDtypeStruct((rows // shares, dim), jnp.float32),
         in_specs=[pl.BlockSpec(memory_space=pltpu.VMEM)],
         out_specs=pl.BlockSpec(memory_space=pltpu.VMEM),
         scratch_shapes=[
-            buffer, buffer, pltpu.VMEM((shares, rows // shares, dim), jnp.float32), buffer,
+            pltpu.VMEM((groups, rows, dim), jnp.float32), buffer,
+            pltpu.VMEM((shares, rows // shares, dim), jnp.float32), buffer,
             pltpu.VMEM((rows, dim), jnp.float32),
             dma((groups,)), dma((groups,)), dma((groups,)), dma((groups,)),
             dma((shares,)), dma((shares,)),

time: 72 us -> 65.2 us (0.906)
  Pallas kernels: 69.5 us -> 62.9 us
    pallas_call x1, Pallas kernels: 12.8 us -> 7.2 us  [backward(): pl.pallas_call(functools.partial(backward_kernel, shares, tile), out_shap...]
    pallas_call x1, Pallas kernels: 24.9 us -> 23.3 us  [gather(): pl.pallas_call(functools.partial(gather_kernel, groups, shares), out_shap...]
where the time goes in v4:
time: 65.2 us; the launch traced here: 64.9 us
  Pallas kernels  62.9 us (96%)
  local copies, waits for them, and re-layouts  1.32 us (2%)
  between operations  0.66 us (1%)
    pallas_call x1, Pallas kernels, gather(): pl.pallas_call(functools.partial(gather_kernel, groups, shares), out_shap...  23.3 us
    pallas_call x1, Pallas kernels, gradient(): pl.pallas_call(functools.partial(gradient_kernel, shares), out_shape=jax....  14 us
    pallas_call x1, Pallas kernels, reduce(): pl.pallas_call(functools.partial(reduce_kernel, groups, shares), out_shap...  13.3 us
    pallas_call x1, Pallas kernels, backward(): pl.pallas_call(functools.partial(backward_kernel, shares, tile), out_shap...  7.2 us
    pallas_call x1, Pallas kernels, forward(): pl.pallas_call(functools.partial(forward_kernel, shares, math.gcd(tokens...  5.06 us
    unnamed x1, local copies, waits for them, and re-layouts  1.32 us

profile of v4, /device:TPU:0, one launch (start us, length us, event | category | flops | bytes accessed | tf_op | source)
XLA Modules:
  0.0 64.9 jit_solution(13099690970648811274)
XLA Ops:
  0.6 23.3 %gather.1 = (f32[4,256,128]{2,1,0:T(8,128)}, bf16[8,128,128]{2,1,0:T(8,128)(2,1)}, bf16[4,2,16,16,128]{4,3,2,1,0:T(8,128)(2,1)}, bf16[4,16,128]{2,1,0:T(8,128)(2,1)}) custom-call(bf16[576,128]{1,0:T(8,128)(2,1)} %bitcast.11, bf16[128,128]{1,0:T(8,128)(2,1)} %idx.1, bf16[128,16,128]{2,1,0:T(8,128)(2,1)} %iq.3, bf16[16,128]{1,0:T(8,128)(2,1)} %bitcast.13, ...), custom_call_target="tpu_custom_call" | custom-call | tf_op jit(solution)/shard_map/gather/pallas_call | solution.py:166
  24.0 5.1 %forward.1 = (f32[128,1024]{1,0:T(8,128)}, f32[32,1024]{1,0:T(8,128)}, bf16[1024,128]{1,0:T(8,128)(2,1)}) custom-call(s32[16]{0:T(128)} %order.3, f32[1024,128]{1,0:T(8,128)} %bitcast.8, bf16[1024,128]{1,0:T(8,128)(2,1)} %bitcast.10, bf16[4,2,16,16,128]{4,3,2,1,0:T(8,128)(2,1)} %get-tuple-element.13.iq, bf16[4,16,128]{2,1,0:T(8,128)(2,1)} %get-tuple-element.14.iw), custom_call_target="tpu_custom_call" | custom-call | tf_op jit(solution)/shard_map/forward/pallas_call | solution.py:276
  29.0 14.0 %gradient.1.grad = bf16[4,2,16,1024]{3,2,1,0:T(8,128)(2,1)} custom-call(f32[128,1024]{1,0:T(8,128)} %get-tuple-element.15.sums, f32[32,1024]{1,0:T(8,128)} %get-tuple-element.16.probs), custom_call_target="tpu_custom_call" | custom-call | tf_op jit(solution)/shard_map/gradient/pallas_call | solution.py:359
  43.1 7.2 %backward.1 = (f32[128,16,128]{2,1,0:T(8,128)}, f32[1024,128]{1,0:T(8,128)}) custom-call(s32[16]{0:T(128)} %order.3, bf16[128,16,128]{2,1,0:T(8,128)(2,1)} %iq.3, bf16[16,128]{1,0:T(8,128)(2,1)} %bitcast.14, bf16[4,2,16,1024]{3,2,1,0:T(8,128)(2,1)} %gradient.1.grad, bf16[1024,128]{1,0:T(8,128)(2,1)} %get-tuple-element.17.idx), custom_call_target="tpu_custom_call" | custom-call | tf_op jit(solution)/shard_map/backward/pallas_call | solution.py:444
  50.3 13.3 %reduce.1 = f32[32,128]{1,0:T(8,128)} custom-call(f32[8,128,128]{2,1,0:T(8,128)} %bitcast.9), custom_call_target="tpu_custom_call" | custom-call | tf_op jit(solution)/shard_map/reduce/pallas_call | solution.py:522
  63.6 1.3 %copy.10 = f32[32,128]{1,0:T(8,128)} copy(f32[32,128]{1,0:T(8,128)} %reduce.1) | data formatting | bytes 32768
